TPU v7x, 32 devices: a whole 2x2x4 slice. The times are simulated.
32 devices in a mesh: groups: 2 (over x), ctx: 16 (over z, y, core).
Axes of the slice: x: 2, y: 2, z: 4, core: 2. Of those that a mesh axis runs over, the one named last changes fastest.
Arguments:
- queries: bfloat16 [16384, 4096], P(('groups', 'ctx')), parts along dimension 0, may hold values from -10 to 10
- keys: bfloat16 [16384, 512], P(('groups', 'ctx')), parts along dimension 0, may hold values from -6 to 6
- values: bfloat16 [16384, 512], P(('groups', 'ctx')), parts along dimension 0, may hold values from -6 to 6
- selected: int32 [32, 2], P(('groups', 'ctx')), parts along dimension 0, may hold values from 0 to 14, as said below
Outputs:
- attended: bfloat16 [16384, 4096], P(('groups', 'ctx')), parts along dimension 0
There are 2 independent parts, one for each index of `groups`. A program takes and returns all parts, laid end to end along the dimension named above; each array names one. Nothing has to cross between parts.
Inputs may be any that keep to these rules, and one draw needn't show every extreme that they name: `selected`: row b names min(b, 2) different blocks below b; its remaining entries equal b.
All inputs are finite; a program needn't handle non-finite values.
Results may differ from a plain program's by a relative error of at most 0.0032.
Values may be sent and summed in bfloat16 or wider, within the bound.
No kernel may reach another device: no remote copies, remote signals or barrier semaphores. Data moves between devices by JAX's collectives and lax.ppermute only.
A program may use at most 128 MiB of HBM per device.

v0:
```python
import math

import jax
import jax.numpy as jnp
from jax import lax
from jax.sharding import PartitionSpec as P

QH = 32
KVH = 4
HD = 128
BLOCK = 512
TOPK = 2


def attend_group(query_rows, key_rows, value_rows, visible):
    group_size = query_rows.shape[1] // HD
    per_head = query_rows.reshape(query_rows.shape[0], group_size, HD)
    scores = jnp.einsum("iqd,jd->qij", per_head, key_rows, preferred_element_type=jnp.float32) * (
        1.0 / math.sqrt(HD)
    )
    scores = jnp.where(visible[None], scores, -1e30)
    row_peak = jnp.max(scores, axis=2, keepdims=True)
    weight = jnp.where(visible[None], jnp.exp(scores - row_peak), 0.0)
    row_total = jnp.sum(weight, axis=2)
    rounded = weight.astype(jnp.bfloat16)
    mixture = jnp.einsum("qij,jd->iqd", rounded, value_rows, preferred_element_type=jnp.float32)
    mixture = mixture / jnp.transpose(row_total)[:, :, None]
    return mixture.astype(jnp.bfloat16).reshape(query_rows.shape[0], group_size * HD)


def attend_block(query_rows, key_set, value_set, visible):
    columns = QH // KVH * HD

    def one_group(group_index, result):
        group_queries = lax.dynamic_slice_in_dim(query_rows, group_index * columns, columns, 1)
        group_keys = lax.dynamic_slice_in_dim(key_set, group_index * HD, HD, 1)
        group_values = lax.dynamic_slice_in_dim(value_set, group_index * HD, HD, 1)
        produced = attend_group(group_queries, group_keys, group_values, visible)
        return lax.dynamic_update_slice_in_dim(result, produced, group_index * columns, 1)

    return lax.fori_loop(0, KVH, one_group, jnp.zeros(query_rows.shape, jnp.bfloat16))


def per_device(queries, keys, values, selected):
    devices = lax.axis_size("ctx")
    stripe = BLOCK // devices
    columns = keys.shape[1]
    local_blocks = selected.shape[0]
    requests = lax.all_gather(selected, "ctx", axis=0, tiled=True)
    banded_keys, banded_values = (
        lax.all_to_all(
            keys.reshape(local_blocks, devices, stripe, columns),
            "ctx",
            split_axis=1,
            concat_axis=0,
            tiled=True,
        ),
        lax.all_to_all(
            values.reshape(local_blocks, devices, stripe, columns),
            "ctx",
            split_axis=1,
            concat_axis=0,
            tiled=True,
        ),
    )
    banded_keys = banded_keys.reshape(devices * local_blocks, stripe, columns)
    banded_values = banded_values.reshape(devices * local_blocks, stripe, columns)
    slot_keys = []
    slot_values = []
    for slot_index in range(TOPK):
        wanted = requests[:, slot_index]
        send_keys = jnp.take(banded_keys, wanted, axis=0).reshape(
            devices, local_blocks, stripe, columns
        )
        send_values = jnp.take(banded_values, wanted, axis=0).reshape(
            devices, local_blocks, stripe, columns
        )
        arrived_keys, arrived_values = (
            lax.all_to_all(send_keys, "ctx", split_axis=0, concat_axis=2, tiled=True),
            lax.all_to_all(send_values, "ctx", split_axis=0, concat_axis=2, tiled=True),
        )
        slot_keys.append(arrived_keys.reshape(local_blocks, BLOCK, columns))
        slot_values.append(arrived_values.reshape(local_blocks, BLOCK, columns))
    fetched_keys = jnp.stack(slot_keys, axis=1)
    fetched_values = jnp.stack(slot_values, axis=1)
    first_block = lax.axis_index("ctx") * local_blocks
    causal = jnp.arange(BLOCK)[:, None] >= jnp.arange(BLOCK)[None, :]
    block_index = first_block + 0
    live_slots = selected[0] < block_index
    slot_visible = jnp.broadcast_to(jnp.repeat(live_slots, BLOCK)[None, :], (BLOCK, TOPK * BLOCK))
    visible = jnp.concatenate([causal, slot_visible], axis=1)
    key_set = jnp.concatenate([keys, fetched_keys[0].reshape(TOPK * BLOCK, columns)], axis=0)
    value_set = jnp.concatenate([values, fetched_values[0].reshape(TOPK * BLOCK, columns)], axis=0)
    outputs = attend_block(queries, key_set, value_set, visible)
    return outputs


def solution(mesh):
    in_specs = (
        P(("groups", "ctx"), None),
        P(("groups", "ctx"), None),
        P(("groups", "ctx"), None),
        P(("groups", "ctx"), None),
    )
    out_specs = P(("groups", "ctx"), None)
    return jax.shard_map(
        per_device, mesh=mesh, in_specs=in_specs, out_specs=out_specs, check_vma=False
    )
```

profile of v0, /device:TPU:0, one launch (start us, length us, event | category | flops | bytes accessed | tf_op | source)
XLA Modules:
  0.0 232.7 jit_solution(8591654225935993900)
XLA Ops:
  0.0 21.7 %all_to_all.66 = bf16[1,16,32,512]{3,2,0,1:T(8,128)(2,1)S(1)} all-to-all(bf16[1,16,32,512]{3,2,0,1:T(8,128)(2,1)} %bitcast.93), channel_id=1, replica_groups=mesh['groups'=2,'ctx'=16] {'ctx'}, dimensions={1} | all-to-all | bytes 1048576 | tf_op jit(solution)/shard_map/all_to_all | solution.py:51
  21.7 4.2 %all-to-all-start = ((bf16[1,16,32,512]{3,2,0,1:T(8,128)(2,1)}), bf16[1,16,32,512]{3,2,0,1:T(8,128)(2,1)S(1)}, u32[]{:S(2)}, u32[]{:S(2)}) async-start(bf16[1,16,32,512]{3,2,0,1:T(8,128)(2,1)} %bitcast.92), calls=%async_computation | async-start | bytes 1048576 | tf_op jit(solution)/shard_map/all_to_all | solution.py:58
  25.9 24.9 %all-gather = s32[16,1,2]{2,1,0:T(1,128)S(1)} all-gather(s32[1,1,2]{2,1,0:T(1,128)} %bitcast.97), channel_id=1, replica_groups=mesh['groups'=2,'ctx'=16] {'ctx'}, dimensions={0}, use_global_device_ids=true | all-gather | bytes 136 | tf_op jit(solution)/shard_map/all_gather | solution.py:49
  53.1 17.3 %all_to_all.67 = bf16[16,1,32,512]{3,2,1,0:T(8,128)(2,1)S(1)} all-to-all(bf16[16,1,32,512]{3,2,1,0:T(8,128)(2,1)S(1)} %get-tuple-element.150), channel_id=1, replica_groups=mesh['groups'=2,'ctx'=16] {'ctx'}, dimensions={0} | all-to-all | bytes 1048576 | tf_op jit(solution)/shard_map/all_to_all | solution.py:79
  70.3 4.4 %all-to-all-start.2 = ((bf16[16,1,32,512]{3,2,1,0:T(8,128)(2,1)}), bf16[16,1,32,512]{3,2,1,0:T(8,128)(2,1)}, u32[]{:S(2)}, u32[]{:S(2)}) async-start(bf16[16,1,32,512]{3,2,1,0:T(8,128)(2,1)} %get-tuple-element.151), calls=%async_computation.2 | async-start | bytes 1048576 | tf_op jit(solution)/shard_map/all_to_all | solution.py:80
  76.9 12.1 %all-to-all-done.2 = bf16[16,1,32,512]{3,2,1,0:T(8,128)(2,1)} async-done(((bf16[16,1,32,512]{3,2,1,0:T(8,128)(2,1)}), bf16[16,1,32,512]{3,2,1,0:T(8,128)(2,1)}, u32[]{:S(2)}, u32[]{:S(2)}) %all-to-all-start.2) | async-done | bytes 524320 | tf_op jit(solution)/shard_map/all_to_all | solution.py:80
  89.0 18.2 %all_to_all.68 = bf16[16,1,32,512]{3,2,1,0:T(8,128)(2,1)S(1)} all-to-all(bf16[16,1,32,512]{3,2,1,0:T(8,128)(2,1)S(1)} %get-tuple-element.149), channel_id=1, replica_groups=mesh['groups'=2,'ctx'=16] {'ctx'}, dimensions={0} | all-to-all | bytes 1048576 | tf_op jit(solution)/shard_map/all_to_all | solution.py:80
  107.2 4.3 %all-to-all-start.4 = ((bf16[16,1,32,512]{3,2,1,0:T(8,128)(2,1)}), bf16[16,1,32,512]{3,2,1,0:T(8,128)(2,1)}, u32[]{:S(2)}, u32[]{:S(2)}) async-start(bf16[16,1,32,512]{3,2,1,0:T(8,128)(2,1)} %get-tuple-element.148), calls=%async_computation.4 | async-start | bytes 1048576 | tf_op jit(solution)/shard_map/all_to_all | solution.py:79
  112.7 1.2 pad_add_fusion
  113.9 1.1 pad_maximum_fusion.2
  115.6 10.1 %all-to-all-done.4 = bf16[16,1,32,512]{3,2,1,0:T(8,128)(2,1)} async-done(((bf16[16,1,32,512]{3,2,1,0:T(8,128)(2,1)}), bf16[16,1,32,512]{3,2,1,0:T(8,128)(2,1)}, u32[]{:S(2)}, u32[]{:S(2)}) %all-to-all-start.4) | async-done | bytes 524320 | tf_op jit(solution)/shard_map/all_to_all | solution.py:79
  125.8 1.1 pad_maximum_fusion.3
  126.9 1.2 pad_maximum_fusion.1
  128.2 1.3 pad_maximum_fusion
  129.4 2.5 %broadcast_in_dim.68.clone = bf16[512,4096]{1,0:T(8,128)(2,1)} broadcast(bf16[]{:T(256)} %constant.80.clone.1), dimensions={} | broadcast | bytes 4194306 | tf_op jit(solution)/shard_map/broadcast_in_dim | solution.py:41
  132.0 100.8 %while.13 = (s32[]{:T(128)}, bf16[512,4096]{1,0:T(8,128)(2,1)}, bf16[1536,512]{0,1:T(8,128)(2,1)}, pred[512,1536]{0,1:T(8,128)(4,1)S(1)}, bf16[1536,512]{1,0:T(8...) while((s32[]{:T(128)}, bf16[512,4096]{1,0:T(8,128)(2,1)}, ...), condition=%wide.region_3.5_spmd, body=%wide.region_0.4_spmd.sunk | while | flops 3260024320 | bytes 38043880 | solution.py:41
  132.0 1.3 constant_dynamic-slice_fusion.2
  133.8 15.2 %fusion.44 = (f32[8,512]{1,0:T(8,128)S(1)}, bf16[8,512,1536]{1,2,0:T(8,128)(2,1)}) fusion(pred[512,1536]{0,1:T(8,128)(4,1)S(1)} %get-tuple-element.222, bf16[512,8,128]{0,2,1:T(8,128)(2,1)S(1)} %bitcast.84, bf16[1536,512]{1,0:T(8,128)(2,1)} %get-tuple-element.223, s32[]{:T(128)S(6)} %select_n.72), kind=kOutput, calls=%fused_computation.45.clone.1 | convolution fusion | flops 1648363008 | bytes 15613956 | tf_op jit(solution)/shard_map/while/body/eval_jaxpr/sub | solution.py:23
  149.0 6.5 %fusion.45 = bf16[512,8,128]{0,2,1:T(8,128)(2,1)S(1)} fusion(bf16[8,512,1536]{1,2,0:T(8,128)(2,1)} %get-tuple-element.193, f32[512,8]{0,1:T(8,128)S(1)} %bitcast.98, bf16[1536,512]{0,1:T(8,128)(2,1)} %get-tuple-element.221, s32[]{:T(128)S(6)} %select_n.72), kind=kOutput, calls=%fused_computation.14.clone.1 | convolution fusion | flops 1611661312 | bytes 14041092 | tf_op jit(solution)/shard_map/while/body/eval_jaxpr/qij,jd->iqd/dot_general | solution.py:26
  156.1 1.0 constant_dynamic-update-slice_fusion.2
  157.2 1.3 constant_dynamic-slice_fusion.2
  159.0 15.2 %fusion.44 = (f32[8,512]{1,0:T(8,128)S(1)}, bf16[8,512,1536]{1,2,0:T(8,128)(2,1)}) fusion(pred[512,1536]{0,1:T(8,128)(4,1)S(1)} %get-tuple-element.222, bf16[512,8,128]{0,2,1:T(8,128)(2,1)S(1)} %bitcast.84, bf16[1536,512]{1,0:T(8,128)(2,1)} %get-tuple-element.223, s32[]{:T(128)S(6)} %select_n.72), kind=kOutput, calls=%fused_computation.45.clone.1 | convolution fusion | flops 1648363008 | bytes 15613956 | tf_op jit(solution)/shard_map/while/body/eval_jaxpr/sub | solution.py:23
  174.2 6.5 %fusion.45 = bf16[512,8,128]{0,2,1:T(8,128)(2,1)S(1)} fusion(bf16[8,512,1536]{1,2,0:T(8,128)(2,1)} %get-tuple-element.193, f32[512,8]{0,1:T(8,128)S(1)} %bitcast.98, bf16[1536,512]{0,1:T(8,128)(2,1)} %get-tuple-element.221, s32[]{:T(128)S(6)} %select_n.72), kind=kOutput, calls=%fused_computation.14.clone.1 | convolution fusion | flops 1611661312 | bytes 14041092 | tf_op jit(solution)/shard_map/while/body/eval_jaxpr/qij,jd->iqd/dot_general | solution.py:26
  181.3 1.0 constant_dynamic-update-slice_fusion.2
  182.4 1.3 constant_dynamic-slice_fusion.2
  184.2 15.2 %fusion.44 = (f32[8,512]{1,0:T(8,128)S(1)}, bf16[8,512,1536]{1,2,0:T(8,128)(2,1)}) fusion(pred[512,1536]{0,1:T(8,128)(4,1)S(1)} %get-tuple-element.222, bf16[512,8,128]{0,2,1:T(8,128)(2,1)S(1)} %bitcast.84, bf16[1536,512]{1,0:T(8,128)(2,1)} %get-tuple-element.223, s32[]{:T(128)S(6)} %select_n.72), kind=kOutput, calls=%fused_computation.45.clone.1 | convolution fusion | flops 1648363008 | bytes 15613956 | tf_op jit(solution)/shard_map/while/body/eval_jaxpr/sub | solution.py:23
  199.4 6.5 %fusion.45 = bf16[512,8,128]{0,2,1:T(8,128)(2,1)S(1)} fusion(bf16[8,512,1536]{1,2,0:T(8,128)(2,1)} %get-tuple-element.193, f32[512,8]{0,1:T(8,128)S(1)} %bitcast.98, bf16[1536,512]{0,1:T(8,128)(2,1)} %get-tuple-element.221, s32[]{:T(128)S(6)} %select_n.72), kind=kOutput, calls=%fused_computation.14.clone.1 | convolution fusion | flops 1611661312 | bytes 14041092 | tf_op jit(solution)/shard_map/while/body/eval_jaxpr/qij,jd->iqd/dot_general | solution.py:26
  206.5 1.0 constant_dynamic-update-slice_fusion.2
  207.5 1.3 constant_dynamic-slice_fusion.2
  209.4 15.2 %fusion.44 = (f32[8,512]{1,0:T(8,128)S(1)}, bf16[8,512,1536]{1,2,0:T(8,128)(2,1)}) fusion(pred[512,1536]{0,1:T(8,128)(4,1)S(1)} %get-tuple-element.222, bf16[512,8,128]{0,2,1:T(8,128)(2,1)S(1)} %bitcast.84, bf16[1536,512]{1,0:T(8,128)(2,1)} %get-tuple-element.223, s32[]{:T(128)S(6)} %select_n.72), kind=kOutput, calls=%fused_computation.45.clone.1 | convolution fusion | flops 1648363008 | bytes 15613956 | tf_op jit(solution)/shard_map/while/body/eval_jaxpr/sub | solution.py:23
  224.6 6.5 %fusion.45 = bf16[512,8,128]{0,2,1:T(8,128)(2,1)S(1)} fusion(bf16[8,512,1536]{1,2,0:T(8,128)(2,1)} %get-tuple-element.193, f32[512,8]{0,1:T(8,128)S(1)} %bitcast.98, bf16[1536,512]{0,1:T(8,128)(2,1)} %get-tuple-element.221, s32[]{:T(128)S(6)} %select_n.72), kind=kOutput, calls=%fused_computation.14.clone.1 | convolution fusion | flops 1611661312 | bytes 14041092 | tf_op jit(solution)/shard_map/while/body/eval_jaxpr/qij,jd->iqd/dot_general | solution.py:26
  231.7 1.0 constant_dynamic-update-slice_fusion.2
  (36 shorter events, 10.4 us)
Async XLA Ops:
  21.7 29.8 %all-to-all-start = ((bf16[1,16,32,512]{3,2,0,1:T(8,128)(2,1)}), bf16[1,16,32,512]{3,2,0,1:T(8,128)(2,1)S(1)}, u32[]{:S(2)}, u32[]{:S(2)}) async-start(bf16[1,16,32,512]{3,2,0,1:T(8,128)(2,1)} %bitcast.92), calls=%async_computation | async-start | bytes 1048576 | tf_op jit(solution)/shard_map/all_to_all | solution.py:58
  53.1 58.4 %copy-start = (bf16[512,512]{1,0:T(8,128)(2,1)S(1)}, bf16[512,512]{1,0:T(8,128)(2,1)}, u32[]{:S(2)}) copy-start(bf16[512,512]{1,0:T(8,128)(2,1)} %param.10) | copy-start | bytes 1572868
  70.3 42.2 %copy-start.4 = (s32[1,2]{1,0:T(1,128)S(1)}, s32[1,2]{1,0:T(1,128)}, u32[]{:S(2)}) copy-start(s32[1,2]{1,0:T(1,128)} %param.11) | copy-start | bytes 28
  70.3 18.7 %all-to-all-start.2 = ((bf16[16,1,32,512]{3,2,1,0:T(8,128)(2,1)}), bf16[16,1,32,512]{3,2,1,0:T(8,128)(2,1)}, u32[]{:S(2)}, u32[]{:S(2)}) async-start(bf16[16,1,32,512]{3,2,1,0:T(8,128)(2,1)} %get-tuple-element.151), calls=%async_computation.2 | async-start | bytes 1048576 | tf_op jit(solution)/shard_map/all_to_all | solution.py:80
  107.2 18.5 %all-to-all-start.4 = ((bf16[16,1,32,512]{3,2,1,0:T(8,128)(2,1)}), bf16[16,1,32,512]{3,2,1,0:T(8,128)(2,1)}, u32[]{:S(2)}, u32[]{:S(2)}) async-start(bf16[16,1,32,512]{3,2,1,0:T(8,128)(2,1)} %get-tuple-element.148), calls=%async_computation.4 | async-start | bytes 1048576 | tf_op jit(solution)/shard_map/all_to_all | solution.py:79
  111.5 15.4 %copy-start.1 = (bf16[512,512]{1,0:T(8,128)(2,1)S(1)}, bf16[512,512]{1,0:T(8,128)(2,1)}, u32[]{:S(2)}) copy-start(bf16[512,512]{1,0:T(8,128)(2,1)} %param.9) | copy-start | bytes 1572868
  115.6 12.5 %copy-start.2 = (bf16[512,512]{0,1:T(8,128)(2,1)S(1)}, bf16[512,512]{0,1:T(8,128)(2,1)}, u32[]{:S(2)}) copy-start(bf16[512,512]{0,1:T(8,128)(2,1)} %copy.23) | copy-start | bytes 1572868
  128.2 3.8 %copy-start.3 = (pred[512,1536]{0,1:T(8,128)(4,1)S(1)}, pred[512,1536]{0,1:T(8,128)(4,1)}, u32[]{:S(2)}) copy-start(pred[512,1536]{0,1:T(8,128)(4,1)} %pad_add_fusion) | copy-start | bytes 2359300
where the time goes:
time: 234 us; the launch traced here: 233 us
  matrix products  87 us (37%)
  blocking collectives  82.1 us (35%)
  waiting for transfers between devices  22.3 us (10%)
  local copies, waits for them, and re-layouts  20.3 us (9%)
  starting transfers between devices  12.8 us (5%)
  other arithmetic  8.02 us (3%)
    sub x4, matrix products, attend_group(): weight = jnp.where(visible[None], jnp.exp(scores - row_peak), 0.0)  60.9 us
    dot_general x4, matrix products, attend_group(): jnp.einsum('qij,jd->iqd', rounded, value_rows, preferred_element_type=jnp...  26.1 us
    all_gather x1, blocking collectives, per_device(): requests = lax.all_gather(selected, 'ctx', axis=0, tiled=True)  24.9 us
    all_to_all x1, blocking collectives, per_device(): lax.all_to_all(keys.reshape(local_blocks, devices, stripe, columns), 'ctx...  21.7 us
    all_to_all x1, blocking collectives, per_device(): lax.all_to_all(send_values, 'ctx', split_axis=0, concat_axis=2, tiled=True)  18.2 us
    all_to_all x1, blocking collectives, per_device(): lax.all_to_all(send_keys, 'ctx', split_axis=0, concat_axis=2, tiled=True)  17.3 us
    all_to_all x1, waiting for transfers between devices, per_device(): lax.all_to_all(send_values, 'ctx', split_axis=0, concat_axis=2, tiled=True)  12.1 us
    all_to_all x1, waiting for transfers between devices, per_device(): lax.all_to_all(send_keys, 'ctx', split_axis=0, concat_axis=2, tiled=True)  10.1 us
  transfers between devices with their start and end apart: 3, of which 2 were waited for; matrix products, arithmetic and copies ran while one was open for 3% of the time, Pallas kernels for 0%

commit v1 on v0

v1 whole, which is shorter than its diff:
```python
import math

import jax
import jax.numpy as jnp
from jax import lax
from jax.experimental import pallas as pl
from jax.experimental.pallas import tpu as pltpu
from jax.sharding import Mesh
from jax.sharding import PartitionSpec as P


QH = 32
KVH = 4
HD = 128
BLOCK = 512
TOPK = 2
GROUP = QH // KVH
EXPONENT_SCALE = math.log2(math.e) / math.sqrt(HD)
QUERIES = 256
ONES = 16
FIRST = ((0, 1, 2, 3),)
CHUNKS = ((0,), (1,), (2,), (3,))
HEADS = 4


def attend_kernel(dead_ref, q_ref, ko_ref, vo_ref, ks_ref, vs_ref, *rest):
    out_ref, k_all, v_t = rest[-3:]

    @pl.when(pl.program_id(1) == 0)
    def _():
        k_all[:BLOCK] = ko_ref[...]
        v_t[:HD, :BLOCK] = vo_ref[...].T
        for s in range(TOPK):
            at = slice(BLOCK * (1 + s), BLOCK * (2 + s))
            k_all[at] = ks_ref[:, s].reshape(BLOCK, HD)
            v_t[:HD, at] = vs_ref[:, s].reshape(BLOCK, HD).T
        v_t[HD:, :] = jnp.ones((ONES, (TOPK + 1) * BLOCK), jnp.bfloat16)

    drop = [0.0] + [dead_ref[s] for s in range(TOPK)]

    def place(unit):
        h, r = unit
        return slice(r * QUERIES, (r + 1) * QUERIES), slice(h * HD, (h + 1) * HD)

    def scores(unit):
        own = (unit[1] + 1) * QUERIES
        spans = [(0, own)] + [(BLOCK * (1 + s), BLOCK * (2 + s)) for s in range(TOPK)]
        q = q_ref[place(unit)]
        score = [
            lax.dot_general(k_all[a:b], q, (((1,), (1,)), ((), ())), preferred_element_type=jnp.float32)
            for a, b in spans
        ]
        u = lax.broadcasted_iota(jnp.int32, (QUERIES, QUERIES), 0)
        t = lax.broadcasted_iota(jnp.int32, (QUERIES, QUERIES), 1)
        last = jnp.where(u <= t, score[0][own - QUERIES :], -1e30)
        score[0] = jnp.concatenate([score[0][: own - QUERIES], last], axis=0) if own > QUERIES else last
        return spans, score

    def finish(unit, spans, score):
        peak = jnp.max(score[0], axis=0, keepdims=True)
        for s in range(1, TOPK + 1):
            peak = jnp.maximum(peak, jnp.max(score[s], axis=0, keepdims=True) - drop[s])
        total = None
        for (a, b), x, d in zip(spans, score, drop):
            weight = jnp.exp2((x - (peak + d)) * EXPONENT_SCALE).astype(jnp.bfloat16)
            part = jnp.dot(v_t[:, a:b], weight, preferred_element_type=jnp.float32)
            total = part if total is None else total + part
        out_ref[place(unit)] = (total[:HD] / total[HD : HD + 1]).T.astype(jnp.bfloat16)

    units = [(h, r) for h in range(HEADS) for r in range(BLOCK // QUERIES)]
    current = scores(units[0])
    for at, unit in enumerate(units):
        following = scores(units[at + 1]) if at + 1 < len(units) else None
        finish(unit, *current)
        current = following


def attend(dead, queries, keys, values, arrived, heads, previous):
    count, first = len(heads), heads[0]
    sources, _, stripe, _ = arrived.shape
    steps = GROUP // HEADS
    block = (sources, TOPK, stripe, HD)
    in_specs = [
        pl.BlockSpec(memory_space=pltpu.SMEM),
        pl.BlockSpec((BLOCK, HEADS * HD), lambda g, h: (0, (first + g) * steps + h)),
        pl.BlockSpec((BLOCK, HD), lambda g, h: (0, first + g)),
        pl.BlockSpec((BLOCK, HD), lambda g, h: (0, first + g)),
        pl.BlockSpec(block, lambda g, h: (0, 0, 0, g)),
        pl.BlockSpec(block, lambda g, h: (0, 0, 0, count + g)),
    ]
    args = [dead, queries, keys, values, arrived, arrived]
    aliases = {}
    if previous is not None:
        in_specs.append(pl.BlockSpec(memory_space=pl.ANY))
        args.append(previous)
        aliases = {len(args) - 1: 0}
    pairs = BLOCK * (TOPK + 1) * BLOCK * GROUP * count
    return pl.pallas_call(
        attend_kernel,
        out_shape=jax.ShapeDtypeStruct(queries.shape, jnp.bfloat16),
        grid=(count, steps),
        in_specs=in_specs,
        out_specs=pl.BlockSpec((BLOCK, HEADS * HD), lambda g, h: (0, (first + g) * steps + h)),
        scratch_shapes=[
            pltpu.VMEM(((TOPK + 1) * BLOCK, HD), jnp.bfloat16),
            pltpu.VMEM((HD + ONES, (TOPK + 1) * BLOCK), jnp.bfloat16),
        ],
        input_output_aliases=aliases,
        cost_estimate=pl.CostEstimate(
            flops=4 * pairs * HD, transcendentals=pairs, bytes_accessed=4 * BLOCK * HD * GROUP * count
        ),
    )(*args)


def after(x, *others):
    return lax.optimization_barrier((x, *others))[0]


def whole(queries, keys, values, selected):
    peers = lax.axis_size("peer")
    stripe = BLOCK // peers
    half, peer = lax.axis_index("half"), lax.axis_index("peer")

    def exchange(x):
        return lax.all_to_all(x, "peer", split_axis=0, concat_axis=0, tiled=True)

    def columns(x, heads):
        return x[:, heads[0] * HD : (heads[-1] + 1) * HD]

    banded = []
    for heads in FIRST:
        both = jnp.concatenate([columns(keys, heads), columns(values, heads)], axis=1)
        banded.append(exchange(both.reshape(peers, stripe, both.shape[1])))
    rows = lax.broadcasted_iota(jnp.int32, (peers, TOPK), 0)
    requests = jnp.where(rows == peer, selected, 0)
    step = 1
    while step < peers:
        pairs = [(i, i ^ step) for i in range(peers)]
        requests = requests + lax.ppermute(requests, "peer", pairs)
        step *= 2
    place = jnp.where(requests // peers == half, peers, 0) + requests % peers
    place = place.reshape(-1)
    arrived = []
    lower = None
    for heads in CHUNKS:
        for group, band in zip(FIRST, banded):
            if heads[0] in group:
                n, width = len(group), HD * len(heads)
                a = (heads[0] - group[0]) * HD
                mine = jnp.concatenate([band[..., a : a + width], band[..., n * HD + a : n * HD + a + width]], axis=-1)
        if lower is not None:
            mine = after(mine, lower)
        lower = lax.ppermute(mine, "half", [(0, 1)])
        table = jnp.concatenate([lower, mine], axis=0)
        send = jnp.take(table, place, axis=0, mode="clip").reshape(peers, TOPK, stripe, table.shape[-1])
        arrived.append(exchange(send))
    block = half * peers + peer
    dead = jnp.where(selected[0] < block, 0.0, 1e30).astype(jnp.float32)
    outputs = None
    for heads, got in zip(CHUNKS, arrived):
        outputs = attend(dead, queries, keys, values, got, heads, outputs)
    return outputs


def solution(mesh):
    groups, ctx = mesh.devices.shape
    halves = 2 if ctx % 2 == 0 else 1
    inner = Mesh(mesh.devices.reshape(groups, halves, ctx // halves), ("groups", "half", "peer"))
    spec = P(("groups", "half", "peer"), None)
    return jax.shard_map(whole, mesh=inner, in_specs=(spec,) * 4, out_specs=spec, check_vma=False)
```

time: 234 us -> 151 us (0.65)
  matrix products: 87 us -> 0 us
  blocking collectives: 82.1 us -> 0 us
  starting transfers between devices: 12.8 us -> 62.6 us
  Pallas kernels: 0 us -> 39.4 us
  waiting for transfers between devices: 22.3 us -> 38.3 us
  local copies, waits for them, and re-layouts: 20.3 us -> 6.7 us
  other arithmetic: 8.02 us -> 3.38 us
    sub x4 -> x0, matrix products: 60.9 us -> none  [attend_group(): weight = jnp.where(visible[None], jnp.exp(scores - row_peak), 0.0)]
    all_to_all x3 -> x0, blocking collectives: 57.2 us -> none  [the longest x1 21.7 us: per_device(): lax.all_to_all(keys.reshape(local_blocks, devices, stripe, columns), 'ctx...]
    pallas_call x0 -> x4, Pallas kernels: none -> 39.4 us  [attend(): pl.pallas_call(attend_kernel, out_shape=jax.ShapeDtypeStruct(queries.shap...]
    ppermute x0 -> x7, waiting for transfers between devices: none -> 38.3 us  [the longest x4 26.1 us: whole(): lower = lax.ppermute(mine, 'half', [(0, 1)])]
    dot_general x4 -> x0, matrix products: 26.1 us -> none  [attend_group(): jnp.einsum('qij,jd->iqd', rounded, value_rows, preferred_element_type=jnp...]
    all_to_all x3 -> x5, starting transfers between devices: 12.8 us -> 38.5 us  [exchange(): return lax.all_to_all(x, 'peer', split_axis=0, concat_axis=0, tiled=True)]
    all_gather x1 -> x0, blocking collectives: 24.9 us -> none  [per_device(): requests = lax.all_gather(selected, 'ctx', axis=0, tiled=True)]
    ppermute x0 -> x7, starting transfers between devices: none -> 24.1 us  [the longest x4 20.4 us: whole(): lower = lax.ppermute(mine, 'half', [(0, 1)])]
  transfers between devices with their start and end apart: 3 -> 12, of which waited for: 2 -> 6; matrix products, arithmetic and copies ran while one was open for 3% -> 4% of each run, Pallas kernels for 0% -> 20%
where the time goes in v1:
time: 151 us
  starting transfers between devices  62.6 us (41%)
  Pallas kernels  39.4 us (26%)
  waiting for transfers between devices  38.3 us (25%)
  local copies, waits for them, and re-layouts  6.7 us (4%)
  other arithmetic  3.38 us (2%)
    pallas_call x4, Pallas kernels, attend(): pl.pallas_call(attend_kernel, out_shape=jax.ShapeDtypeStruct(queries.shap...  39.4 us
    all_to_all x5, starting transfers between devices, exchange(): return lax.all_to_all(x, 'peer', split_axis=0, concat_axis=0, tiled=True)  38.5 us
    ppermute x4, waiting for transfers between devices, whole(): lower = lax.ppermute(mine, 'half', [(0, 1)])  26.1 us
    ppermute x4, starting transfers between devices, whole(): lower = lax.ppermute(mine, 'half', [(0, 1)])  20.4 us
    ppermute x3, waiting for transfers between devices, whole(): requests = requests + lax.ppermute(requests, 'peer', pairs)  12.1 us
    gather x4, local copies, waits for them, and re-layouts, whole(): jnp.take(table, place, axis=0, mode='clip')  5.52 us
    ppermute x3, starting transfers between devices, whole(): requests = requests + lax.ppermute(requests, 'peer', pairs)  3.69 us
  transfers between devices with their start and end apart: 12, of which 6 were waited for; matrix products, arithmetic and copies ran while one was open for 4% of the time, Pallas kernels for 20%

profile of v1, /device:TPU:0, one launch (start us, length us, event | category | flops | bytes accessed | tf_op | source)
XLA Modules:
  0.0 150.6 jit_solution(123234545747844799)
XLA Ops:
  0.0 2.3 %pad_maximum_fusion = bf16[512,1024]{1,0:T(8,128)(2,1)} fusion(bf16[512,512]{1,0:T(8,128)(2,1)} %vo_ref.7, bf16[512,512]{1,0:T(8,128)(2,1)} %ko_ref.7), kind=kLoop, calls=%fused_computation.4 | loop fusion | flops 2097152 | bytes 2097152 | tf_op jit(solution)/shard_map/concatenate | solution.py:132
  2.3 5.3 %all-to-all-start = ((bf16[8,64,1024]{2,1,0:T(8,128)(2,1)}), bf16[8,64,1024]{2,1,0:T(8,128)(2,1)S(1)}, u32[]{:S(2)}, u32[]{:S(2)}) async-start(bf16[8,64,1024]{2,1,0:T(8,128)(2,1)} %bitcast.1), calls=%async_computation | async-start | bytes 2097152 | tf_op jit(solution)/shard_map/all_to_all | solution.py:125
  7.7 0.5 collective-permute-start.4
  8.2 1.0 collective-permute-done.4
  9.2 1.7 %collective-permute-start.5 = (s32[8,2]{1,0:T(8,128)S(1)}, s32[8,2]{1,0:T(8,128)S(1)}, u32[]{:S(2)}, u32[]{:S(2)}) collective-permute-start(s32[8,2]{1,0:T(8,128)S(1)} %fusion.4), channel_id=1, source_target_pairs={{0,2},{1,3},{2,0},{3,1},{4,6},{5,7},{6,4},{7,5},{8,10},{9,11},{10,... | collective-permute-start | bytes 200 | tf_op jit(solution)/shard_map/ppermute | solution.py:139
  10.9 11.2 %collective-permute-done.5 = s32[8,2]{1,0:T(8,128)S(1)} collective-permute-done((s32[8,2]{1,0:T(8,128)S(1)}, s32[8,2]{1,0:T(8,128)S(1)}, u32[]{:S(2)}, u32[]{:S(2)}) %collective-permute-start.5) | collective-permute-done | bytes 96 | tf_op jit(solution)/shard_map/ppermute | solution.py:139
  22.1 0.1 fusion.6
  22.2 1.5 collective-permute-start.6
  23.6 0.3 fusion.5
  24.0 4.5 %collective-permute-start = (bf16[8,64,256]{2,1,0:T(8,128)(2,1)S(1)}, bf16[8,64,256]{2,1,0:T(8,128)(2,1)S(1)}, u32[]{:S(2)}, u32[]{:S(2)}) collective-permute-start(bf16[8,64,256]{2,1,0:T(8,128)(2,1)S(1)} %pad_maximum_fusion.7), channel_id=1, source_target_pairs={{0,8},{1,9},{2,10},{3,11},{4,12},{5,13},{6,14},{7,15},{16,24},{17,... | collective-permute-start | bytes 786440 | tf_op jit(solution)/shard_map/ppermute | solution.py:153
  28.5 0.1 reshape.24
  28.6 4.9 %collective-permute-done = bf16[8,64,256]{2,1,0:T(8,128)(2,1)S(1)} collective-permute-done((bf16[8,64,256]{2,1,0:T(8,128)(2,1)S(1)}, bf16[8,64,256]{2,1,0:T(8,128)(2,1)S(1)}, u32[]{:S(2)}, u32[]{:S(2)}) %collective-permute-start) | collective-permute-done | bytes 262176 | tf_op jit(solution)/shard_map/ppermute | solution.py:153
  33.5 1.4 gather_fusion.3
  34.9 7.6 %all-to-all-start.4 = ((bf16[8,2,64,256]{3,2,1,0:T(8,128)(2,1)}), bf16[8,2,64,256]{3,2,1,0:T(8,128)(2,1)S(1)}, u32[]{:S(2)}, u32[]{:S(2)}) async-start(bf16[8,2,64,256]{3,2,1,0:T(8,128)(2,1)} %bitcast.5), calls=%async_computation.4 | async-start | bytes 1048576 | tf_op jit(solution)/shard_map/all_to_all | solution.py:125
  42.6 5.3 %collective-permute-start.1 = (bf16[8,64,256]{2,1,0:T(8,128)(2,1)S(1)}, bf16[8,64,256]{2,1,0:T(8,128)(2,1)S(1)}, u32[]{:S(2)}, u32[]{:S(2)}) collective-permute-start(bf16[8,64,256]{2,1,0:T(8,128)(2,1)S(1)} %pad_maximum_fusion.6), channel_id=1, source_target_pairs={{0,8},{1,9},{2,10},{3,11},{4,12},{5,13},{6,14},{7,15},{16,24},{17,... | collective-permute-start | bytes 786440 | tf_op jit(solution)/shard_map/ppermute | solution.py:153
  47.9 7.1 %collective-permute-done.1 = bf16[8,64,256]{2,1,0:T(8,128)(2,1)S(1)} collective-permute-done((bf16[8,64,256]{2,1,0:T(8,128)(2,1)S(1)}, bf16[8,64,256]{2,1,0:T(8,128)(2,1)S(1)}, u32[]{:S(2)}, u32[]{:S(2)}) %collective-permute-start.1) | collective-permute-done | bytes 262176 | tf_op jit(solution)/shard_map/ppermute | solution.py:153
  55.0 1.4 gather_fusion.2
  56.4 8.5 %all-to-all-start.3 = ((bf16[8,2,64,256]{3,2,1,0:T(8,128)(2,1)}), bf16[8,2,64,256]{3,2,1,0:T(8,128)(2,1)S(1)}, u32[]{:S(2)}, u32[]{:S(2)}) async-start(bf16[8,2,64,256]{3,2,1,0:T(8,128)(2,1)} %bitcast.4), calls=%async_computation.3 | async-start | bytes 1048576 | tf_op jit(solution)/shard_map/all_to_all | solution.py:125
  65.0 5.3 %collective-permute-start.2 = (bf16[8,64,256]{2,1,0:T(8,128)(2,1)S(1)}, bf16[8,64,256]{2,1,0:T(8,128)(2,1)S(1)}, u32[]{:S(2)}, u32[]{:S(2)}) collective-permute-start(bf16[8,64,256]{2,1,0:T(8,128)(2,1)S(1)} %pad_maximum_fusion.5), channel_id=1, source_target_pairs={{0,8},{1,9},{2,10},{3,11},{4,12},{5,13},{6,14},{7,15},{16,24},{17,... | collective-permute-start | bytes 786440 | tf_op jit(solution)/shard_map/ppermute | solution.py:153
  70.3 7.1 %collective-permute-done.2 = bf16[8,64,256]{2,1,0:T(8,128)(2,1)S(1)} collective-permute-done((bf16[8,64,256]{2,1,0:T(8,128)(2,1)S(1)}, bf16[8,64,256]{2,1,0:T(8,128)(2,1)S(1)}, u32[]{:S(2)}, u32[]{:S(2)}) %collective-permute-start.2) | collective-permute-done | bytes 262176 | tf_op jit(solution)/shard_map/ppermute | solution.py:153
  77.4 1.4 gather_fusion.1
  78.8 8.5 %all-to-all-start.2 = ((bf16[8,2,64,256]{3,2,1,0:T(8,128)(2,1)}), bf16[8,2,64,256]{3,2,1,0:T(8,128)(2,1)S(1)}, u32[]{:S(2)}, u32[]{:S(2)}) async-start(bf16[8,2,64,256]{3,2,1,0:T(8,128)(2,1)} %bitcast.3), calls=%async_computation.2 | async-start | bytes 1048576 | tf_op jit(solution)/shard_map/all_to_all | solution.py:125
  87.4 5.3 %collective-permute-start.3 = (bf16[8,64,256]{2,1,0:T(8,128)(2,1)S(1)}, bf16[8,64,256]{2,1,0:T(8,128)(2,1)S(1)}, u32[]{:S(2)}, u32[]{:S(2)}) collective-permute-start(bf16[8,64,256]{2,1,0:T(8,128)(2,1)S(1)} %pad_maximum_fusion.4), channel_id=1, source_target_pairs={{0,8},{1,9},{2,10},{3,11},{4,12},{5,13},{6,14},{7,15},{16,24},{17,... | collective-permute-start | bytes 786440 | tf_op jit(solution)/shard_map/ppermute | solution.py:153
  92.7 7.1 %collective-permute-done.3 = bf16[8,64,256]{2,1,0:T(8,128)(2,1)S(1)} collective-permute-done((bf16[8,64,256]{2,1,0:T(8,128)(2,1)S(1)}, bf16[8,64,256]{2,1,0:T(8,128)(2,1)S(1)}, u32[]{:S(2)}, u32[]{:S(2)}) %collective-permute-start.3) | collective-permute-done | bytes 262176 | tf_op jit(solution)/shard_map/ppermute | solution.py:153
  99.8 1.4 gather_fusion
  101.2 8.6 %all-to-all-start.1 = ((bf16[8,2,64,256]{3,2,1,0:T(8,128)(2,1)}), bf16[8,2,64,256]{3,2,1,0:T(8,128)(2,1)S(1)}, u32[]{:S(2)}, u32[]{:S(2)}) async-start(bf16[8,2,64,256]{3,2,1,0:T(8,128)(2,1)} %bitcast.2), calls=%async_computation.1 | async-start | bytes 1048576 | tf_op jit(solution)/shard_map/all_to_all | solution.py:125
  109.8 0.5 compare_select_fusion.dead_ref
  110.3 9.8 %shard_map.46.rest_0_ = bf16[512,4096]{1,0:T(8,128)(2,1)} custom-call(f32[2]{0:T(128)} %compare_select_fusion.dead_ref, bf16[512,4096]{1,0:T(8,128)(2,1)} %q_ref.7, bf16[512,512]{1,0:T(8,128)(2,1)} %ko_ref.7, bf16[512,512]{1,0:T(8,128)(2,1)} %vo_ref.7, bf16[8,2,64,256]{3,2,1,0:T(8,128)(2,1)} %copy-done.3, bf16[8,2,64,256]{3,2,1,0:T(8,128)(2,1)} %copy-done.3), custom_call_target="tpu_custom_call" | custom-call | flops 3221225472 | bytes 2097152 | tf_op jit(solution)/shard_map/pallas_call | solution.py:98
  120.2 9.9 %shard_map.47.rest_0_ = bf16[512,4096]{1,0:T(8,128)(2,1)} custom-call(f32[2]{0:T(128)} %compare_select_fusion.dead_ref, bf16[512,4096]{1,0:T(8,128)(2,1)} %q_ref.7, bf16[512,512]{1,0:T(8,128)(2,1)} %ko_ref.7, bf16[512,512]{1,0:T(8,128)(2,1)} %vo_ref.7, bf16[8,2,64,256]{3,2,1,0:T(8,128)(2,1)} %copy-done, ...), custom_call_target="tpu_custom_call", output_to_operand_aliasing={{}: (6, {})} | custom-call | flops 3221225472 | bytes 2097152 | tf_op jit(solution)/shard_map/pallas_call | solution.py:98
  130.0 9.9 %shard_map.48.rest_0_ = bf16[512,4096]{1,0:T(8,128)(2,1)} custom-call(f32[2]{0:T(128)} %compare_select_fusion.dead_ref, bf16[512,4096]{1,0:T(8,128)(2,1)} %q_ref.7, bf16[512,512]{1,0:T(8,128)(2,1)} %ko_ref.7, bf16[512,512]{1,0:T(8,128)(2,1)} %vo_ref.7, bf16[8,2,64,256]{3,2,1,0:T(8,128)(2,1)} %copy-done.1, ...), custom_call_target="tpu_custom_call", output_to_operand_aliasing={{}: (6, {})} | custom-call | flops 3221225472 | bytes 2097152 | tf_op jit(solution)/shard_map/pallas_call | solution.py:98
  139.9 0.8 copy-done.2
  140.7 9.8 %shard_map.49 = bf16[512,4096]{1,0:T(8,128)(2,1)} custom-call(f32[2]{0:T(128)} %compare_select_fusion.dead_ref, bf16[512,4096]{1,0:T(8,128)(2,1)} %q_ref.7, bf16[512,512]{1,0:T(8,128)(2,1)} %ko_ref.7, bf16[512,512]{1,0:T(8,128)(2,1)} %vo_ref.7, bf16[8,2,64,256]{3,2,1,0:T(8,128)(2,1)} %copy-done.2, ...), custom_call_target="tpu_custom_call", output_to_operand_aliasing={{}: (6, {})} | custom-call | flops 3221225472 | bytes 2097152 | tf_op jit(solution)/shard_map/pallas_call | solution.py:98
  (28 shorter events, 0.5 us)
Async XLA Ops:
  0.0 7.6 %copy-start.4 = (s32[1,2]{1,0:T(1,128)S(1)}, s32[1,2]{1,0:T(1,128)}, u32[]{:S(2)}) copy-start(s32[1,2]{1,0:T(1,128)} %param.7) | copy-start | bytes 28
  2.3 21.3 %all-to-all-start = ((bf16[8,64,1024]{2,1,0:T(8,128)(2,1)}), bf16[8,64,1024]{2,1,0:T(8,128)(2,1)S(1)}, u32[]{:S(2)}, u32[]{:S(2)}) async-start(bf16[8,64,1024]{2,1,0:T(8,128)(2,1)} %bitcast.1), calls=%async_computation | async-start | bytes 2097152 | tf_op jit(solution)/shard_map/all_to_all | solution.py:125
  7.7 1.5 collective-permute-start.4
  9.2 12.9 %collective-permute-start.5 = (s32[8,2]{1,0:T(8,128)S(1)}, s32[8,2]{1,0:T(8,128)S(1)}, u32[]{:S(2)}, u32[]{:S(2)}) collective-permute-start(s32[8,2]{1,0:T(8,128)S(1)} %fusion.4), channel_id=1, source_target_pairs={{0,2},{1,3},{2,0},{3,1},{4,6},{5,7},{6,4},{7,5},{8,10},{9,11},{10,... | collective-permute-start | bytes 200 | tf_op jit(solution)/shard_map/ppermute | solution.py:139
  22.2 6.3 %collective-permute-start.6 = (s32[8,2]{1,0:T(8,128)S(1)}, s32[8,2]{1,0:T(8,128)S(1)}, u32[]{:S(2)}, u32[]{:S(2)}) collective-permute-start(s32[8,2]{1,0:T(8,128)S(1)} %fusion.6), channel_id=1, source_target_pairs={{0,4},{1,5},{2,6},{3,7},{4,0},{5,1},{6,2},{7,3},{8,12},{9,13},{10,... | collective-permute-start | bytes 200 | tf_op jit(solution)/shard_map/ppermute | solution.py:139
  24.0 9.5 %collective-permute-start = (bf16[8,64,256]{2,1,0:T(8,128)(2,1)S(1)}, bf16[8,64,256]{2,1,0:T(8,128)(2,1)S(1)}, u32[]{:S(2)}, u32[]{:S(2)}) collective-permute-start(bf16[8,64,256]{2,1,0:T(8,128)(2,1)S(1)} %pad_maximum_fusion.7), channel_id=1, source_target_pairs={{0,8},{1,9},{2,10},{3,11},{4,12},{5,13},{6,14},{7,15},{16,24},{17,... | collective-permute-start | bytes 786440 | tf_op jit(solution)/shard_map/ppermute | solution.py:153
  34.9 21.5 %all-to-all-start.4 = ((bf16[8,2,64,256]{3,2,1,0:T(8,128)(2,1)}), bf16[8,2,64,256]{3,2,1,0:T(8,128)(2,1)S(1)}, u32[]{:S(2)}, u32[]{:S(2)}) async-start(bf16[8,2,64,256]{3,2,1,0:T(8,128)(2,1)} %bitcast.5), calls=%async_computation.4 | async-start | bytes 1048576 | tf_op jit(solution)/shard_map/all_to_all | solution.py:125
  42.6 12.4 %collective-permute-start.1 = (bf16[8,64,256]{2,1,0:T(8,128)(2,1)S(1)}, bf16[8,64,256]{2,1,0:T(8,128)(2,1)S(1)}, u32[]{:S(2)}, u32[]{:S(2)}) collective-permute-start(bf16[8,64,256]{2,1,0:T(8,128)(2,1)S(1)} %pad_maximum_fusion.6), channel_id=1, source_target_pairs={{0,8},{1,9},{2,10},{3,11},{4,12},{5,13},{6,14},{7,15},{16,24},{17,... | collective-permute-start | bytes 786440 | tf_op jit(solution)/shard_map/ppermute | solution.py:153
  56.4 44.8 %copy-start.3 = (bf16[8,2,64,256]{3,2,1,0:T(8,128)(2,1)}, bf16[8,2,64,256]{3,2,1,0:T(8,128)(2,1)S(1)}, u32[]{:S(2)}) copy-start(bf16[8,2,64,256]{3,2,1,0:T(8,128)(2,1)S(1)} %all-to-all-done.4.ks_ref.vs_ref) | copy-start | bytes 1572868
  56.4 22.4 %all-to-all-start.3 = ((bf16[8,2,64,256]{3,2,1,0:T(8,128)(2,1)}), bf16[8,2,64,256]{3,2,1,0:T(8,128)(2,1)S(1)}, u32[]{:S(2)}, u32[]{:S(2)}) async-start(bf16[8,2,64,256]{3,2,1,0:T(8,128)(2,1)} %bitcast.4), calls=%async_computation.3 | async-start | bytes 1048576 | tf_op jit(solution)/shard_map/all_to_all | solution.py:125
  65.0 12.4 %collective-permute-start.2 = (bf16[8,64,256]{2,1,0:T(8,128)(2,1)S(1)}, bf16[8,64,256]{2,1,0:T(8,128)(2,1)S(1)}, u32[]{:S(2)}, u32[]{:S(2)}) collective-permute-start(bf16[8,64,256]{2,1,0:T(8,128)(2,1)S(1)} %pad_maximum_fusion.5), channel_id=1, source_target_pairs={{0,8},{1,9},{2,10},{3,11},{4,12},{5,13},{6,14},{7,15},{16,24},{17,... | collective-permute-start | bytes 786440 | tf_op jit(solution)/shard_map/ppermute | solution.py:153
  78.8 41.4 %copy-start = (bf16[8,2,64,256]{3,2,1,0:T(8,128)(2,1)}, bf16[8,2,64,256]{3,2,1,0:T(8,128)(2,1)S(1)}, u32[]{:S(2)}) copy-start(bf16[8,2,64,256]{3,2,1,0:T(8,128)(2,1)S(1)} %all-to-all-done.3.ks_ref.vs_ref) | copy-start | bytes 1572868
  78.8 22.4 %all-to-all-start.2 = ((bf16[8,2,64,256]{3,2,1,0:T(8,128)(2,1)}), bf16[8,2,64,256]{3,2,1,0:T(8,128)(2,1)S(1)}, u32[]{:S(2)}, u32[]{:S(2)}) async-start(bf16[8,2,64,256]{3,2,1,0:T(8,128)(2,1)} %bitcast.3), calls=%async_computation.2 | async-start | bytes 1048576 | tf_op jit(solution)/shard_map/all_to_all | solution.py:125
  87.4 12.4 %collective-permute-start.3 = (bf16[8,64,256]{2,1,0:T(8,128)(2,1)S(1)}, bf16[8,64,256]{2,1,0:T(8,128)(2,1)S(1)}, u32[]{:S(2)}, u32[]{:S(2)}) collective-permute-start(bf16[8,64,256]{2,1,0:T(8,128)(2,1)S(1)} %pad_maximum_fusion.4), channel_id=1, source_target_pairs={{0,8},{1,9},{2,10},{3,11},{4,12},{5,13},{6,14},{7,15},{16,24},{17,... | collective-permute-start | bytes 786440 | tf_op jit(solution)/shard_map/ppermute | solution.py:153
  101.2 18.9 %copy-start.1 = (bf16[8,2,64,256]{3,2,1,0:T(8,128)(2,1)}, bf16[8,2,64,256]{3,2,1,0:T(8,128)(2,1)S(1)}, u32[]{:S(2)}) copy-start(bf16[8,2,64,256]{3,2,1,0:T(8,128)(2,1)S(1)} %all-to-all-done.2.ks_ref.vs_ref) | copy-start | bytes 1572868
  101.2 38.7 %all-to-all-start.1 = ((bf16[8,2,64,256]{3,2,1,0:T(8,128)(2,1)}), bf16[8,2,64,256]{3,2,1,0:T(8,128)(2,1)S(1)}, u32[]{:S(2)}, u32[]{:S(2)}) async-start(bf16[8,2,64,256]{3,2,1,0:T(8,128)(2,1)} %bitcast.2), calls=%async_computation.1 | async-start | bytes 1048576 | tf_op jit(solution)/shard_map/all_to_all | solution.py:125
  139.9 0.8 copy-start.2

commit v2 on v1

v2 whole, which is shorter than its diff:
```python
import math

import jax
import jax.numpy as jnp
from jax import lax
from jax.experimental import pallas as pl
from jax.experimental.pallas import tpu as pltpu
from jax.sharding import Mesh
from jax.sharding import PartitionSpec as P


QH = 32
KVH = 4
HD = 128
BLOCK = 512
TOPK = 2
GROUP = QH // KVH
EXPONENT_SCALE = math.log2(math.e) / math.sqrt(HD)
QUERIES = 512
ONES = 16
KEPT = HD + 8
DIGIT = 128
CHUNKS = ((0, 1), (2, 3))
HEADS = 4
STAGED = False
NT = (((1,), (1,)), ((), ()))


def piece(unit):
    h, r = unit
    return slice(r * QUERIES, (r + 1) * QUERIES), slice(h * HD, (h + 1) * HD)


def staggered(units, scores, weigh, finish):
    scored, weighed = {}, {}
    for at in range(len(units) + 2):
        for c in "SEA":
            if c == "S" and at < len(units):
                scored[at] = scores(units[at])
            if c == "E" and 0 <= at - 1 < len(units):
                weighed[at - 1] = weigh(units[at - 1], scored.pop(at - 1))
            if c == "A" and 0 <= at - 2 < len(units):
                finish(units[at - 2], weighed.pop(at - 2))


def units_of(heads):
    return [(h, r) for h in range(heads) for r in range(BLOCK // QUERIES)]


def own_kernel(q_ref, k_ref, v_ref, kept_ref, v_t):
    @pl.when(pl.program_id(1) == 0)
    def _():
        v_t[:HD] = v_ref[...].T
        v_t[HD:] = jnp.ones((ONES, BLOCK), jnp.bfloat16)

    def scores(unit):
        own = (unit[1] + 1) * QUERIES
        x = lax.dot_general(k_ref[:own], q_ref[piece(unit)], NT, preferred_element_type=jnp.float32)
        u = lax.broadcasted_iota(jnp.int32, (QUERIES, QUERIES), 0)
        t = lax.broadcasted_iota(jnp.int32, (QUERIES, QUERIES), 1)
        last = jnp.where(u <= t, x[own - QUERIES :], -1e30)
        return jnp.concatenate([x[: own - QUERIES], last], axis=0) if own > QUERIES else last

    def weigh(unit, x):
        peak = jnp.max(x, axis=0, keepdims=True)
        return peak, jnp.exp2((x - peak) * EXPONENT_SCALE).astype(jnp.bfloat16)

    def finish(unit, held):
        h, r = unit
        peak, weight = held
        total = jnp.dot(v_t[:, : weight.shape[0]], weight, preferred_element_type=jnp.float32)
        at = slice(r * QUERIES, (r + 1) * QUERIES)
        kept_ref[h, :HD, at] = total[:HD]
        row = lax.broadcasted_iota(jnp.int32, (KEPT - HD, QUERIES), 0)
        kept_ref[h, HD:, at] = jnp.where(row == 0, total[HD : HD + KEPT - HD], peak)

    staggered(units_of(HEADS), scores, weigh, finish)


def attend_own(queries, keys, values):
    steps = GROUP // HEADS
    pairs = BLOCK * BLOCK * QH
    return pl.pallas_call(
        own_kernel,
        out_shape=jax.ShapeDtypeStruct((QH, KEPT, BLOCK), jnp.float32),
        grid=(KVH, steps),
        in_specs=[
            pl.BlockSpec((BLOCK, HEADS * HD), lambda g, h: (0, g * steps + h)),
            pl.BlockSpec((BLOCK, HD), lambda g, h: (0, g)),
            pl.BlockSpec((BLOCK, HD), lambda g, h: (0, g)),
        ],
        out_specs=pl.BlockSpec((HEADS, KEPT, BLOCK), lambda g, h: (g * steps + h, 0, 0)),
        scratch_shapes=[pltpu.VMEM((HD + ONES, BLOCK), jnp.bfloat16)],
        cost_estimate=pl.CostEstimate(
            flops=4 * pairs * HD, transcendentals=pairs, bytes_accessed=4 * QH * KEPT * BLOCK
        ),
        name="attend_own",
    )(queries, keys, values)


def slots_kernel(dead_ref, q_ref, kept_ref, ks_ref, vs_ref, *rest):
    out_ref, k_all, v_t = rest[-3:]

    @pl.when(pl.program_id(0) == 0)
    def _():
        for s in range(TOPK):
            at = slice(BLOCK * s, BLOCK * (s + 1))
            k_all[at] = ks_ref[:, s].reshape(BLOCK, HD)
            v_t[:HD, at] = vs_ref[:, s].reshape(BLOCK, HD).T
        v_t[HD:] = jnp.ones((ONES, TOPK * BLOCK), jnp.bfloat16)

    drop = [dead_ref[s] for s in range(TOPK)]
    spans = [(BLOCK * s, BLOCK * (s + 1)) for s in range(TOPK)]

    def scores(unit):
        q = q_ref[piece(unit)]
        return [lax.dot_general(k_all[a:b], q, NT, preferred_element_type=jnp.float32) for a, b in spans]

    def weigh(unit, score):
        h, r = unit
        mine = kept_ref[h, HD + 1 : HD + 2, r * QUERIES : (r + 1) * QUERIES]
        peak = mine
        for x, d in zip(score, drop):
            peak = jnp.maximum(peak, jnp.max(x, axis=0, keepdims=True) - d)
        shrink = jnp.exp2((mine - peak) * EXPONENT_SCALE)
        weights = [
            jnp.exp2((x - (peak + d)) * EXPONENT_SCALE).astype(jnp.bfloat16) for x, d in zip(score, drop)
        ]
        return shrink, weights

    def finish(unit, held):
        h, r = unit
        at = slice(r * QUERIES, (r + 1) * QUERIES)
        shrink, weights = held
        total = None
        for (a, b), weight in zip(spans, weights):
            part = jnp.dot(v_t[:, a:b], weight, preferred_element_type=jnp.float32)
            total = part if total is None else total + part
        mixture = kept_ref[h, :HD, at] * shrink + total[:HD]
        row_total = kept_ref[h, HD : HD + 1, at] * shrink + total[HD : HD + 1]
        out_ref[piece(unit)] = (mixture * (1.0 / row_total)).T.astype(jnp.bfloat16)

    staggered(units_of(HEADS), scores, weigh, finish)


def attend_slots(dead, queries, kept, arrived, head, at, previous):
    sources, _, stripe, width = arrived.shape
    count = width // (2 * HD)
    steps = GROUP // HEADS
    block = (sources, TOPK, stripe, HD)
    in_specs = [
        pl.BlockSpec(memory_space=pltpu.SMEM),
        pl.BlockSpec((BLOCK, HEADS * HD), lambda h: (0, head * steps + h)),
        pl.BlockSpec((HEADS, KEPT, BLOCK), lambda h: (head * steps + h, 0, 0)),
        pl.BlockSpec(block, lambda h: (0, 0, 0, at)),
        pl.BlockSpec(block, lambda h: (0, 0, 0, count + at)),
    ]
    args = [dead, queries, kept, arrived, arrived]
    aliases = {}
    if previous is not None:
        in_specs.append(pl.BlockSpec(memory_space=pl.ANY))
        args.append(previous)
        aliases = {len(args) - 1: 0}
    pairs = BLOCK * TOPK * BLOCK * GROUP
    return pl.pallas_call(
        slots_kernel,
        out_shape=jax.ShapeDtypeStruct(queries.shape, jnp.bfloat16),
        grid=(steps,),
        in_specs=in_specs,
        out_specs=pl.BlockSpec((BLOCK, HEADS * HD), lambda h: (0, head * steps + h)),
        scratch_shapes=[
            pltpu.VMEM((TOPK * BLOCK, HD), jnp.bfloat16),
            pltpu.VMEM((HD + ONES, TOPK * BLOCK), jnp.bfloat16),
        ],
        input_output_aliases=aliases,
        cost_estimate=pl.CostEstimate(
            flops=4 * pairs * HD, transcendentals=pairs, bytes_accessed=8 * BLOCK * HD * GROUP
        ),
    )(*args)


def after(x, *others):
    return lax.optimization_barrier((x, *others))[0]


def whole(queries, keys, values, selected):
    halves, peers = lax.axis_size("half"), lax.axis_size("peer")
    stripe = BLOCK // peers
    half, peer = lax.axis_index("half"), lax.axis_index("peer")

    def exchange(x):
        return lax.all_to_all(x, "peer", split_axis=0, concat_axis=0, tiled=True)

    def columns(x, heads):
        return x[:, heads[0] * HD : (heads[-1] + 1) * HD]

    digits = jnp.concatenate([selected // DIGIT, selected % DIGIT], axis=1).astype(jnp.bfloat16)
    banded = []
    for at, heads in enumerate(CHUNKS):
        both = jnp.concatenate([columns(keys, heads), columns(values, heads)], axis=1)
        both = both.reshape(peers, stripe, both.shape[1])
        if at == 0:
            asked = jnp.pad(digits, ((0, 15), (0, both.shape[2] - 2 * TOPK)))
            both = jnp.concatenate([both, jnp.broadcast_to(asked, (peers, *asked.shape))], axis=1)
        else:
            both = after(both, banded[0]) if STAGED else both
        banded.append(exchange(both))
    kept = attend_own(queries, keys, values)
    digits = banded[0][:, stripe, : 2 * TOPK].astype(jnp.int32)
    requests = digits[:, :TOPK] * DIGIT + digits[:, TOPK:]
    place = jnp.where(requests // peers == half, peers, 0) + requests % peers
    place = place.reshape(-1)
    arrived = []
    lower = None
    for band in banded:
        mine = band[:, :stripe]
        if lower is not None:
            mine = after(mine, lower)
        lower = lax.ppermute(mine, "half", [(0, 1)]) if halves > 1 else mine
        table = jnp.concatenate([lower, mine], axis=0)
        send = jnp.take(table, place, axis=0, mode="clip").reshape(peers, TOPK, *mine.shape[1:])
        arrived.append(exchange(send))
    block = half * peers + peer
    dead = jnp.where(selected[0] < block, 0.0, 1e30).astype(jnp.float32)
    outputs = None
    for heads, got in zip(CHUNKS, arrived):
        for at, head in enumerate(heads):
            outputs = attend_slots(dead, queries, kept, got, head, at, outputs)
    return outputs


def solution(mesh):
    groups, ctx = mesh.devices.shape
    halves = 2 if ctx % 2 == 0 else 1
    inner = Mesh(mesh.devices.reshape(groups, halves, ctx // halves), ("groups", "half", "peer"))
    spec = P(("groups", "half", "peer"), None)
    return jax.shard_map(whole, mesh=inner, in_specs=(spec,) * 4, out_specs=spec, check_vma=False)
```

time: 151 us -> 138 us (0.914)
  starting transfers between devices: 62.6 us -> 40.8 us
  Pallas kernels: 39.4 us -> 46.1 us
  waiting for transfers between devices: 38.3 us -> 40.8 us
    ppermute x7 -> x2, starting transfers between devices: 24.1 us -> 9.83 us  [whole(): lower = lax.ppermute(mine, 'half', [(0, 1)]) if halves > 1 else mine]
    all_to_all x5 -> x4, waiting for transfers between devices: 0.01 us -> 9.44 us  [exchange(): return lax.all_to_all(x, 'peer', split_axis=0, concat_axis=0, tiled=True)]
    all_to_all x5 -> x4, starting transfers between devices: 38.5 us -> 31 us  [exchange(): return lax.all_to_all(x, 'peer', split_axis=0, concat_axis=0, tiled=True)]
    ppermute x7 -> x2, waiting for transfers between devices: 38.3 us -> 31.4 us  [whole(): lower = lax.ppermute(mine, 'half', [(0, 1)]) if halves > 1 else mine]
    pallas_call x4 -> x5, Pallas kernels: 39.4 us -> 46.1 us  [the longest x4 33.1 us: attend_slots(): pl.pallas_call(slots_kernel, out_shape=jax.ShapeDtypeStruct(queries.shape...]
    gather x4 -> x2, local copies, waits for them, and re-layouts: 5.52 us -> 3.17 us  [whole(): jnp.take(table, place, axis=0, mode='clip')]
  transfers between devices with their start and end apart: 12 -> 6, of which waited for: 6 -> 3; matrix products, arithmetic and copies ran while one was open for 4% -> 4% of each run, Pallas kernels for 20% -> 22%
where the time goes in v2:
time: 138 us; the launch traced here: 137 us
  Pallas kernels  46.1 us (33%)
  starting transfers between devices  40.8 us (30%)
  waiting for transfers between devices  40.8 us (30%)
  local copies, waits for them, and re-layouts  5.72 us (4%)
  other arithmetic  3.3 us (2%)
    pallas_call x4, Pallas kernels, attend_slots(): pl.pallas_call(slots_kernel, out_shape=jax.ShapeDtypeStruct(queries.shape...  33.1 us
    ppermute x2, waiting for transfers between devices, whole(): lower = lax.ppermute(mine, 'half', [(0, 1)]) if halves > 1 else mine  31.4 us
    all_to_all x4, starting transfers between devices, exchange(): return lax.all_to_all(x, 'peer', split_axis=0, concat_axis=0, tiled=True)  31 us
    pallas_call x1, Pallas kernels, attend_own(): pl.pallas_call(own_kernel, out_shape=jax.ShapeDtypeStruct((QH, KEPT, BLOC...  13 us
    ppermute x2, starting transfers between devices, whole(): lower = lax.ppermute(mine, 'half', [(0, 1)]) if halves > 1 else mine  9.83 us
    all_to_all x4, waiting for transfers between devices, exchange(): return lax.all_to_all(x, 'peer', split_axis=0, concat_axis=0, tiled=True)  9.44 us
    gather x2, local copies, waits for them, and re-layouts, whole(): jnp.take(table, place, axis=0, mode='clip')  3.17 us
  transfers between devices with their start and end apart: 6, of which 3 were waited for; matrix products, arithmetic and copies ran while one was open for 4% of the time, Pallas kernels for 22%

profile of v2, /device:TPU:0, one launch (start us, length us, event | category | flops | bytes accessed | tf_op | source)
XLA Modules:
  0.0 136.9 jit_solution(6025127457621616422)
XLA Ops:
  0.0 0.7 fusion.9
  0.7 0.1 fusion.5
  0.7 1.3 fusion.10
  2.1 0.9 pad_maximum_fusion.2
  3.0 5.3 %all-to-all-start.1 = ((bf16[8,80,512]{2,1,0:T(8,128)(2,1)}), bf16[8,80,512]{2,1,0:T(8,128)(2,1)S(1)}, u32[]{:S(2)}, u32[]{:S(2)}) async-start(bf16[8,80,512]{2,1,0:T(8,128)(2,1)} %pad_maximum_fusion.2), calls=%async_computation.1 | async-start | bytes 1310720 | tf_op jit(solution)/shard_map/all_to_all | solution.py:192
  8.2 0.8 pad_maximum_fusion.3
  9.1 9.4 %all-to-all-done.1 = bf16[8,80,512]{2,1,0:T(8,128)(2,1)S(1)} async-done(((bf16[8,80,512]{2,1,0:T(8,128)(2,1)}), bf16[8,80,512]{2,1,0:T(8,128)(2,1)S(1)}, u32[]{:S(2)}, u32[]{:S(2)}) %all-to-all-start.1) | async-done | bytes 655392 | tf_op jit(solution)/shard_map/all_to_all | solution.py:192
  18.5 3.5 %all-to-all-start = ((bf16[8,64,512]{2,1,0:T(8,128)(2,1)}), bf16[8,64,512]{2,1,0:T(8,128)(2,1)S(1)}, u32[]{:S(2)}, u32[]{:S(2)}) async-start(bf16[8,64,512]{2,1,0:T(8,128)(2,1)} %bitcast.1), calls=%async_computation | async-start | bytes 1048576 | tf_op jit(solution)/shard_map/all_to_all | solution.py:192
  22.0 0.1 copy.20
  22.2 4.5 %collective-permute-start = (bf16[8,64,512]{2,1,0:T(8,128)(2,1)S(1)}, bf16[8,64,512]{2,1,0:T(8,128)(2,1)S(1)}, u32[]{:S(2)}, u32[]{:S(2)}) collective-permute-start(bf16[8,64,512]{2,1,0:T(8,128)(2,1)S(1)} %slice.36), channel_id=1, source_target_pairs={{0,8},{1,9},{2,10},{3,11},{4,12},{5,13},{6,14},{7,15},{16,24},{17,... | collective-permute-start | bytes 1572872 | tf_op jit(solution)/shard_map/ppermute | solution.py:219
  26.7 0.1 copy.19
  26.8 0.1 reshape.56
  26.9 13.1 %collective-permute-done = bf16[8,64,512]{2,1,0:T(8,128)(2,1)S(1)} collective-permute-done((bf16[8,64,512]{2,1,0:T(8,128)(2,1)S(1)}, bf16[8,64,512]{2,1,0:T(8,128)(2,1)S(1)}, u32[]{:S(2)}, u32[]{:S(2)}) %collective-permute-start) | collective-permute-done | bytes 524320 | tf_op jit(solution)/shard_map/ppermute | solution.py:219
  40.0 0.1 pad_maximum_fusion.1
  40.1 1.6 %gather_fusion.1 = bf16[16,64,512]{2,1,0:T(8,128)(2,1)} fusion(bf16[16,64,512]{2,1,0:T(8,128)(2,1)S(1)} %pad_maximum_fusion.1, s32[1024]{0:T(1024)S(1)} %pad_clamp_fusion), kind=kCustom, calls=%fused_computation.1 | custom fusion | bytes 2097216 | tf_op jit(solution)/shard_map/jit(_take)/gather | solution.py:221
  41.6 0.0 all-to-all-done
  41.6 13.7 %all-to-all-start.3 = ((bf16[8,2,64,512]{3,2,1,0:T(8,128)(2,1)}), bf16[8,2,64,512]{3,2,1,0:T(8,128)(2,1)S(1)}, u32[]{:S(2)}, u32[]{:S(2)}) async-start(bf16[8,2,64,512]{3,2,1,0:T(8,128)(2,1)} %bitcast.6), calls=%async_computation.3 | async-start | bytes 2097152 | tf_op jit(solution)/shard_map/all_to_all | solution.py:192
  55.3 5.3 %collective-permute-start.1 = (bf16[8,64,512]{2,1,0:T(8,128)(2,1)S(1)}, bf16[8,64,512]{2,1,0:T(8,128)(2,1)S(1)}, u32[]{:S(2)}, u32[]{:S(2)}) collective-permute-start(bf16[8,64,512]{2,1,0:T(8,128)(2,1)S(1)} %all-to-all-done), channel_id=1, source_target_pairs={{0,8},{1,9},{2,10},{3,11},{4,12},{5,13},{6,14},{7,15},{16,24},{17,... | collective-permute-start | bytes 1572872 | tf_op jit(solution)/shard_map/ppermute | solution.py:219
  60.6 18.4 %collective-permute-done.1 = bf16[8,64,512]{2,1,0:T(8,128)(2,1)S(1)} collective-permute-done((bf16[8,64,512]{2,1,0:T(8,128)(2,1)S(1)}, bf16[8,64,512]{2,1,0:T(8,128)(2,1)S(1)}, u32[]{:S(2)}, u32[]{:S(2)}) %collective-permute-start.1) | collective-permute-done | bytes 524320 | tf_op jit(solution)/shard_map/ppermute | solution.py:219
  79.0 0.1 pad_maximum_fusion
  79.1 1.6 %gather_fusion = bf16[16,64,512]{2,1,0:T(8,128)(2,1)} fusion(bf16[16,64,512]{2,1,0:T(8,128)(2,1)S(1)} %pad_maximum_fusion, s32[1024]{0:T(1024)S(1)} %pad_clamp_fusion), kind=kCustom, calls=%fused_computation | custom fusion | bytes 2097216 | tf_op jit(solution)/shard_map/jit(_take)/gather | solution.py:221
  80.6 0.0 all-to-all-done.3.ks_ref.vs_ref
  80.6 8.5 %all-to-all-start.2 = ((bf16[8,2,64,512]{3,2,1,0:T(8,128)(2,1)}), bf16[8,2,64,512]{3,2,1,0:T(8,128)(2,1)S(1)}, u32[]{:S(2)}, u32[]{:S(2)}) async-start(bf16[8,2,64,512]{3,2,1,0:T(8,128)(2,1)} %bitcast.5), calls=%async_computation.2 | async-start | bytes 2097152 | tf_op jit(solution)/shard_map/all_to_all | solution.py:192
  89.2 0.0 copy-done.2
  89.2 0.6 fusion.7.dead_ref
  89.8 13.0 %attend_own.1.kept_ref = f32[32,136,512]{2,1,0:T(8,128)} custom-call(bf16[512,4096]{1,0:T(8,128)(2,1)} %q_ref.9, bf16[512,512]{1,0:T(8,128)(2,1)} %k_ref.1, bf16[512,512]{1,0:T(8,128)(2,1)} %v_ref.1), custom_call_target="tpu_custom_call" | custom-call | flops 4294967296 | bytes 8912896 | tf_op jit(solution)/shard_map/attend_own/pallas_call | solution.py:83
  102.8 8.2 %shard_map.46.rest_0_ = bf16[512,4096]{1,0:T(8,128)(2,1)} custom-call(f32[2]{0:T(128)} %fusion.7.dead_ref, bf16[512,4096]{1,0:T(8,128)(2,1)} %q_ref.9, f32[32,136,512]{2,1,0:T(8,128)} %attend_own.1.kept_ref, bf16[8,2,64,512]{3,2,1,0:T(8,128)(2,1)} %copy-done, bf16[8,2,64,512]{3,2,1,0:T(8,128)(2,1)} %copy-done), custom_call_target="tpu_custom_call" | custom-call | flops 2147483648 | bytes 4194304 | tf_op jit(solution)/shard_map/pallas_call | solution.py:165
  111.0 8.2 %shard_map.47.rest_0_ = bf16[512,4096]{1,0:T(8,128)(2,1)} custom-call(f32[2]{0:T(128)} %fusion.7.dead_ref, bf16[512,4096]{1,0:T(8,128)(2,1)} %q_ref.9, f32[32,136,512]{2,1,0:T(8,128)} %attend_own.1.kept_ref, bf16[8,2,64,512]{3,2,1,0:T(8,128)(2,1)} %copy-done, bf16[8,2,64,512]{3,2,1,0:T(8,128)(2,1)} %copy-done, ...), custom_call_target="tpu_custom_call", output_to_operand_aliasing={{}: (5, {})} | custom-call | flops 2147483648 | bytes 4194304 | tf_op jit(solution)/shard_map/pallas_call | solution.py:165
  119.3 0.0 all-to-all-done.2.ks_ref.vs_ref
  119.3 1.0 copy-done.1
  120.2 8.2 %shard_map.48.rest_0_ = bf16[512,4096]{1,0:T(8,128)(2,1)} custom-call(f32[2]{0:T(128)} %fusion.7.dead_ref, bf16[512,4096]{1,0:T(8,128)(2,1)} %q_ref.9, f32[32,136,512]{2,1,0:T(8,128)} %attend_own.1.kept_ref, bf16[8,2,64,512]{3,2,1,0:T(8,128)(2,1)} %copy-done.1, bf16[8,2,64,512]{3,2,1,0:T(8,128)(2,1)} %copy-done.1, ...), custom_call_target="tpu_custom_call", output_to_operand_aliasing={{}: (5, {})} | custom-call | flops 2147483648 | bytes 4194304 | tf_op jit(solution)/shard_map/pallas_call | solution.py:165
  128.5 8.4 %shard_map.49 = bf16[512,4096]{1,0:T(8,128)(2,1)} custom-call(f32[2]{0:T(128)} %fusion.7.dead_ref, bf16[512,4096]{1,0:T(8,128)(2,1)} %q_ref.9, f32[32,136,512]{2,1,0:T(8,128)} %attend_own.1.kept_ref, bf16[8,2,64,512]{3,2,1,0:T(8,128)(2,1)} %copy-done.1, bf16[8,2,64,512]{3,2,1,0:T(8,128)(2,1)} %copy-done.1, ...), custom_call_target="tpu_custom_call", output_to_operand_aliasing={{}: (5, {})} | custom-call | flops 2147483648 | bytes 4194304 | tf_op jit(solution)/shard_map/pallas_call | solution.py:165
  (11 shorter events, 0.1 us)
Async XLA Ops:
  3.0 15.5 %all-to-all-start.1 = ((bf16[8,80,512]{2,1,0:T(8,128)(2,1)}), bf16[8,80,512]{2,1,0:T(8,128)(2,1)S(1)}, u32[]{:S(2)}, u32[]{:S(2)}) async-start(bf16[8,80,512]{2,1,0:T(8,128)(2,1)} %pad_maximum_fusion.2), calls=%async_computation.1 | async-start | bytes 1310720 | tf_op jit(solution)/shard_map/all_to_all | solution.py:192
  18.5 23.1 %all-to-all-start = ((bf16[8,64,512]{2,1,0:T(8,128)(2,1)}), bf16[8,64,512]{2,1,0:T(8,128)(2,1)S(1)}, u32[]{:S(2)}, u32[]{:S(2)}) async-start(bf16[8,64,512]{2,1,0:T(8,128)(2,1)} %bitcast.1), calls=%async_computation | async-start | bytes 1048576 | tf_op jit(solution)/shard_map/all_to_all | solution.py:192
  22.2 17.8 %collective-permute-start = (bf16[8,64,512]{2,1,0:T(8,128)(2,1)S(1)}, bf16[8,64,512]{2,1,0:T(8,128)(2,1)S(1)}, u32[]{:S(2)}, u32[]{:S(2)}) collective-permute-start(bf16[8,64,512]{2,1,0:T(8,128)(2,1)S(1)} %slice.36), channel_id=1, source_target_pairs={{0,8},{1,9},{2,10},{3,11},{4,12},{5,13},{6,14},{7,15},{16,24},{17,... | collective-permute-start | bytes 1572872 | tf_op jit(solution)/shard_map/ppermute | solution.py:219
  41.6 47.6 %copy-start.2 = (s32[1,2]{1,0:T(1,128)S(1)}, s32[1,2]{1,0:T(1,128)}, u32[]{:S(2)}) copy-start(s32[1,2]{1,0:T(1,128)} %param.7) | copy-start | bytes 28
  41.6 39.0 %all-to-all-start.3 = ((bf16[8,2,64,512]{3,2,1,0:T(8,128)(2,1)}), bf16[8,2,64,512]{3,2,1,0:T(8,128)(2,1)S(1)}, u32[]{:S(2)}, u32[]{:S(2)}) async-start(bf16[8,2,64,512]{3,2,1,0:T(8,128)(2,1)} %bitcast.6), calls=%async_computation.3 | async-start | bytes 2097152 | tf_op jit(solution)/shard_map/all_to_all | solution.py:192
  55.3 23.7 %collective-permute-start.1 = (bf16[8,64,512]{2,1,0:T(8,128)(2,1)S(1)}, bf16[8,64,512]{2,1,0:T(8,128)(2,1)S(1)}, u32[]{:S(2)}, u32[]{:S(2)}) collective-permute-start(bf16[8,64,512]{2,1,0:T(8,128)(2,1)S(1)} %all-to-all-done), channel_id=1, source_target_pairs={{0,8},{1,9},{2,10},{3,11},{4,12},{5,13},{6,14},{7,15},{16,24},{17,... | collective-permute-start | bytes 1572872 | tf_op jit(solution)/shard_map/ppermute | solution.py:219
  80.6 22.1 %copy-start = (bf16[8,2,64,512]{3,2,1,0:T(8,128)(2,1)}, bf16[8,2,64,512]{3,2,1,0:T(8,128)(2,1)S(1)}, u32[]{:S(2)}) copy-start(bf16[8,2,64,512]{3,2,1,0:T(8,128)(2,1)S(1)} %all-to-all-done.3.ks_ref.vs_ref) | copy-start | bytes 3145732
  80.6 38.6 %all-to-all-start.2 = ((bf16[8,2,64,512]{3,2,1,0:T(8,128)(2,1)}), bf16[8,2,64,512]{3,2,1,0:T(8,128)(2,1)S(1)}, u32[]{:S(2)}, u32[]{:S(2)}) async-start(bf16[8,2,64,512]{3,2,1,0:T(8,128)(2,1)} %bitcast.5), calls=%async_computation.2 | async-start | bytes 2097152 | tf_op jit(solution)/shard_map/all_to_all | solution.py:192
  119.3 1.0 copy-start.1

commit v3 on v2

--- a/solution.py
+++ b/solution.py
@@ -22,7 +22,6 @@
 DIGIT = 128
 CHUNKS = ((0, 1), (2, 3))
 HEADS = 4
-STAGED = False
 NT = (((1,), (1,)), ((), ()))
 
 
@@ -77,31 +76,31 @@
     staggered(units_of(HEADS), scores, weigh, finish)
 
 
-def attend_own(queries, keys, values):
+def attend_own(queries, keys, values, heads):
     steps = GROUP // HEADS
-    pairs = BLOCK * BLOCK * QH
+    count, first = len(heads), heads[0]
+    pairs = BLOCK * BLOCK * GROUP * count
     return pl.pallas_call(
         own_kernel,
-        out_shape=jax.ShapeDtypeStruct((QH, KEPT, BLOCK), jnp.float32),
-        grid=(KVH, steps),
+        out_shape=jax.ShapeDtypeStruct((GROUP * count, KEPT, BLOCK), jnp.float32),
+        grid=(count, steps),
         in_specs=[
-            pl.BlockSpec((BLOCK, HEADS * HD), lambda g, h: (0, g * steps + h)),
-            pl.BlockSpec((BLOCK, HD), lambda g, h: (0, g)),
-            pl.BlockSpec((BLOCK, HD), lambda g, h: (0, g)),
+            pl.BlockSpec((BLOCK, HEADS * HD), lambda g, h: (0, (first + g) * steps + h)),
+            pl.BlockSpec((BLOCK, HD), lambda g, h: (0, first + g)),
+            pl.BlockSpec((BLOCK, HD), lambda g, h: (0, first + g)),
         ],
         out_specs=pl.BlockSpec((HEADS, KEPT, BLOCK), lambda g, h: (g * steps + h, 0, 0)),
         scratch_shapes=[pltpu.VMEM((HD + ONES, BLOCK), jnp.bfloat16)],
         cost_estimate=pl.CostEstimate(
-            flops=4 * pairs * HD, transcendentals=pairs, bytes_accessed=4 * QH * KEPT * BLOCK
+            flops=4 * pairs * HD, transcendentals=pairs, bytes_accessed=4 * GROUP * count * KEPT * BLOCK
         ),
-        name="attend_own",
     )(queries, keys, values)
 
 
 def slots_kernel(dead_ref, q_ref, kept_ref, ks_ref, vs_ref, *rest):
     out_ref, k_all, v_t = rest[-3:]
 
-    @pl.when(pl.program_id(0) == 0)
+    @pl.when(pl.program_id(1) == 0)
     def _():
         for s in range(TOPK):
             at = slice(BLOCK * s, BLOCK * (s + 1))
@@ -143,17 +142,17 @@
     staggered(units_of(HEADS), scores, weigh, finish)
 
 
-def attend_slots(dead, queries, kept, arrived, head, at, previous):
-    sources, _, stripe, width = arrived.shape
-    count = width // (2 * HD)
+def attend_slots(dead, queries, kept, arrived, heads, previous):
+    sources, _, stripe, _ = arrived.shape
+    count, first = len(heads), heads[0]
     steps = GROUP // HEADS
     block = (sources, TOPK, stripe, HD)
     in_specs = [
         pl.BlockSpec(memory_space=pltpu.SMEM),
-        pl.BlockSpec((BLOCK, HEADS * HD), lambda h: (0, head * steps + h)),
-        pl.BlockSpec((HEADS, KEPT, BLOCK), lambda h: (head * steps + h, 0, 0)),
-        pl.BlockSpec(block, lambda h: (0, 0, 0, at)),
-        pl.BlockSpec(block, lambda h: (0, 0, 0, count + at)),
+        pl.BlockSpec((BLOCK, HEADS * HD), lambda g, h: (0, (first + g) * steps + h)),
+        pl.BlockSpec((HEADS, KEPT, BLOCK), lambda g, h: (g * steps + h, 0, 0)),
+        pl.BlockSpec(block, lambda g, h: (0, 0, 0, g)),
+        pl.BlockSpec(block, lambda g, h: (0, 0, 0, count + g)),
     ]
     args = [dead, queries, kept, arrived, arrived]
     aliases = {}
@@ -161,20 +160,20 @@
         in_specs.append(pl.BlockSpec(memory_space=pl.ANY))
         args.append(previous)
         aliases = {len(args) - 1: 0}
-    pairs = BLOCK * TOPK * BLOCK * GROUP
+    pairs = BLOCK * TOPK * BLOCK * GROUP * count
     return pl.pallas_call(
         slots_kernel,
         out_shape=jax.ShapeDtypeStruct(queries.shape, jnp.bfloat16),
-        grid=(steps,),
+        grid=(count, steps),
         in_specs=in_specs,
-        out_specs=pl.BlockSpec((BLOCK, HEADS * HD), lambda h: (0, head * steps + h)),
+        out_specs=pl.BlockSpec((BLOCK, HEADS * HD), lambda g, h: (0, (first + g) * steps + h)),
         scratch_shapes=[
             pltpu.VMEM((TOPK * BLOCK, HD), jnp.bfloat16),
             pltpu.VMEM((HD + ONES, TOPK * BLOCK), jnp.bfloat16),
         ],
         input_output_aliases=aliases,
         cost_estimate=pl.CostEstimate(
-            flops=4 * pairs * HD, transcendentals=pairs, bytes_accessed=8 * BLOCK * HD * GROUP
+            flops=4 * pairs * HD, transcendentals=pairs, bytes_accessed=8 * BLOCK * HD * GROUP * count
         ),
     )(*args)
 
@@ -184,7 +183,7 @@
 
 
 def whole(queries, keys, values, selected):
-    halves, peers = lax.axis_size("half"), lax.axis_size("peer")
+    peers = lax.axis_size("peer")
     stripe = BLOCK // peers
     half, peer = lax.axis_index("half"), lax.axis_index("peer")
 
@@ -194,44 +193,65 @@
     def columns(x, heads):
         return x[:, heads[0] * HD : (heads[-1] + 1) * HD]
 
-    digits = jnp.concatenate([selected // DIGIT, selected % DIGIT], axis=1).astype(jnp.bfloat16)
+    twin = lax.ppermute(selected, "half", [(0, 1), (1, 0)])
+    numbers = jnp.concatenate([selected, twin], axis=1)
+    digits = jnp.concatenate([numbers // DIGIT, numbers % DIGIT], axis=1).astype(jnp.bfloat16)
     banded = []
     for at, heads in enumerate(CHUNKS):
         both = jnp.concatenate([columns(keys, heads), columns(values, heads)], axis=1)
         both = both.reshape(peers, stripe, both.shape[1])
         if at == 0:
-            asked = jnp.pad(digits, ((0, 15), (0, both.shape[2] - 2 * TOPK)))
+            asked = jnp.pad(digits, ((0, 15), (0, both.shape[2] - 4 * TOPK)))
             both = jnp.concatenate([both, jnp.broadcast_to(asked, (peers, *asked.shape))], axis=1)
-        else:
-            both = after(both, banded[0]) if STAGED else both
         banded.append(exchange(both))
-    kept = attend_own(queries, keys, values)
-    digits = banded[0][:, stripe, : 2 * TOPK].astype(jnp.int32)
-    requests = digits[:, :TOPK] * DIGIT + digits[:, TOPK:]
-    place = jnp.where(requests // peers == half, peers, 0) + requests % peers
-    place = place.reshape(-1)
+    kept = []
+    for heads in CHUNKS:
+        kept.append(attend_own(queries, keys, values, heads))
+    digits = banded[0][:, stripe, : 4 * TOPK].astype(jnp.int32)
+    numbers = digits[:, : 2 * TOPK] * DIGIT + digits[:, 2 * TOPK :]
+    requests = numbers[:, :TOPK]
+    upper = jnp.where(half == 1, requests, numbers[:, TOPK:]).reshape(-1)
+    lanes = jnp.arange(peers, dtype=jnp.int32)
+    needed = jnp.any(upper[:, None] == lanes[None, :], axis=0).astype(jnp.int32)
+    rank = jnp.sum(jnp.where(lanes[:, None] < lanes[None, :], needed[:, None], 0), axis=0)
+    turns = jnp.sum(
+        jnp.where((rank[:, None] == lanes[None, :]) & (needed[:, None] > 0), lanes[:, None], 0), axis=0
+    )
+    room = (peers + 1) // 2
+    more = jnp.sum(needed) > room
+    asked = requests.reshape(-1)
+    turn = jnp.sum(jnp.where(asked[:, None] % peers == lanes[None, :], rank[None, :], 0), axis=1)
+    near = asked // peers == half
     arrived = []
-    lower = None
+    first = None
     for band in banded:
         mine = band[:, :stripe]
-        if lower is not None:
-            mine = after(mine, lower)
-        lower = lax.ppermute(mine, "half", [(0, 1)]) if halves > 1 else mine
-        table = jnp.concatenate([lower, mine], axis=0)
-        send = jnp.take(table, place, axis=0, mode="clip").reshape(peers, TOPK, *mine.shape[1:])
-        arrived.append(exchange(send))
+        front = jnp.take(mine, turns[:room], axis=0, mode="clip")
+        if first is not None:
+            front = after(front, first)
+        first = lax.ppermute(front, "half", [(0, 1)])
+
+        def all_crossed(first, mine):
+            rest = lax.ppermute(jnp.take(mine, turns[room:], axis=0, mode="clip"), "half", [(0, 1)])
+            table = jnp.concatenate([first, rest, mine], axis=0)
+            return jnp.take(table, jnp.where(near, peers + asked % peers, turn), axis=0, mode="clip")
+
+        def few_crossed(first, mine):
+            table = jnp.concatenate([first, mine], axis=0)
+            return jnp.take(table, jnp.where(near, room + asked % peers, turn), axis=0, mode="clip")
+
+        send = lax.cond(more, all_crossed, few_crossed, first, mine)
+        arrived.append(exchange(send.reshape(peers, TOPK, *mine.shape[1:])))
     block = half * peers + peer
     dead = jnp.where(selected[0] < block, 0.0, 1e30).astype(jnp.float32)
     outputs = None
-    for heads, got in zip(CHUNKS, arrived):
-        for at, head in enumerate(heads):
-            outputs = attend_slots(dead, queries, kept, got, head, at, outputs)
+    for at, heads in enumerate(CHUNKS):
+        outputs = attend_slots(dead, queries, kept[at], arrived[at], heads, outputs)
     return outputs
 
 
 def solution(mesh):
     groups, ctx = mesh.devices.shape
-    halves = 2 if ctx % 2 == 0 else 1
-    inner = Mesh(mesh.devices.reshape(groups, halves, ctx // halves), ("groups", "half", "peer"))
+    inner = Mesh(mesh.devices.reshape(groups, 2, ctx // 2), ("groups", "half", "peer"))
     spec = P(("groups", "half", "peer"), None)
     return jax.shard_map(whole, mesh=inner, in_specs=(spec,) * 4, out_specs=spec, check_vma=False)

time: 138 us -> 117 us (0.85)
  waiting for transfers between devices: 40.8 us -> 27.1 us
  starting transfers between devices: 40.8 us -> 34 us
  Pallas kernels: 46.1 us -> 43.3 us
    ppermute x2 -> x3, waiting for transfers between devices: 31.4 us -> 17.7 us  [the longest x2 17.3 us: whole(): first = lax.ppermute(front, 'half', [(0, 1)])]
    all_to_all x4, starting transfers between devices: 31 us -> 20.1 us  [exchange(): return lax.all_to_all(x, 'peer', split_axis=0, concat_axis=0, tiled=True)]
    pallas_call x4 -> x2, Pallas kernels: 33.1 us -> 28.5 us  [attend_slots(): pl.pallas_call(slots_kernel, out_shape=jax.ShapeDtypeStruct(queries.shape...]
    ppermute x2 -> x3, starting transfers between devices: 9.83 us -> 13.9 us  [the longest x2 9.81 us: whole(): first = lax.ppermute(front, 'half', [(0, 1)])]
    pallas_call x1 -> x2, Pallas kernels: 13 us -> 14.8 us  [attend_own(): pl.pallas_call(own_kernel, out_shape=jax.ShapeDtypeStruct((GROUP * count,...]
    gather x2 -> x4, local copies, waits for them, and re-layouts: 3.17 us -> 4.3 us  [the longest x2 3.17 us: few_crossed(): jnp.take(table, jnp.where(near, room + asked % peers, turn), axis=0, mode...]
  transfers between devices with their start and end apart: 6 -> 7, of which waited for: 3 -> 4; matrix products, arithmetic and copies ran while one was open for 4% -> 7% of each run, Pallas kernels for 22% -> 25%
where the time goes in v3:
time: 117 us; the launch traced here: 116 us
  Pallas kernels  43.3 us (37%)
  starting transfers between devices  34 us (29%)
  waiting for transfers between devices  27.1 us (23%)
  local copies, waits for them, and re-layouts  6.77 us (6%)
  other arithmetic  4.48 us (4%)
    pallas_call x2, Pallas kernels, attend_slots(): pl.pallas_call(slots_kernel, out_shape=jax.ShapeDtypeStruct(queries.shape...  28.5 us
    all_to_all x4, starting transfers between devices, exchange(): return lax.all_to_all(x, 'peer', split_axis=0, concat_axis=0, tiled=True)  20.1 us
    ppermute x2, waiting for transfers between devices, whole(): first = lax.ppermute(front, 'half', [(0, 1)])  17.3 us
    pallas_call x2, Pallas kernels, attend_own(): pl.pallas_call(own_kernel, out_shape=jax.ShapeDtypeStruct((GROUP * count,...  14.8 us
    ppermute x2, starting transfers between devices, whole(): first = lax.ppermute(front, 'half', [(0, 1)])  9.81 us
    all_to_all x4, waiting for transfers between devices, exchange(): return lax.all_to_all(x, 'peer', split_axis=0, concat_axis=0, tiled=True)  9.44 us
    ppermute x1, starting transfers between devices, whole(): twin = lax.ppermute(selected, 'half', [(0, 1), (1, 0)])  4.06 us
    gather x2, local copies, waits for them, and re-layouts, few_crossed(): jnp.take(table, jnp.where(near, room + asked % peers, turn), axis=0, mode...  3.17 us
  transfers between devices with their start and end apart: 7, of which 4 were waited for; matrix products, arithmetic and copies ran while one was open for 7% of the time, Pallas kernels for 25%

profile of v3, /device:TPU:0, one launch (start us, length us, event | category | flops | bytes accessed | tf_op | source)
XLA Modules:
  0.0 116.4 jit_solution(9798070635364183400)
XLA Ops:
  0.0 4.1 %collective-permute-start.2 = (s32[1,2]{1,0:T(1,128)}, s32[1,2]{1,0:T(1,128)S(1)}, u32[]{:S(2)}, u32[]{:S(2)}) collective-permute-start(s32[1,2]{1,0:T(1,128)} %param.11), channel_id=1, source_target_pairs={{0,8},{8,0},{1,9},{9,1},{2,10},{10,2},{3,11},{11,3},{4,12},{12,4},... | collective-permute-start | bytes 32 | tf_op jit(solution)/shard_map/ppermute | solution.py:196
  4.1 1.3 %fusion.23 = (bf16[512,256]{1,0:T(8,128)(2,1)S(1)}, bf16[512,256]{1,0:T(8,128)(2,1)S(1)}, bf16[512,256]{1,0:T(8,128)(2,1)S(1)}, bf16[512,256]{1,0:T(8,128)(2,1)S(1)}) fusion(bf16[512,512]{1,0:T(8,128)(2,1)} %k_ref.3, bf16[512,512]{1,0:T(8,128)(2,1)} %v_ref.3), kind=kLoop, calls=%fused_computation.84 | loop fusion | bytes 2097152 | tf_op jit(solution)/shard_map/slice | solution.py:194
  5.4 0.4 collective-permute-done.2
  5.7 0.7 convert_bitcast_fusion
  6.6 0.9 pad_maximum_fusion.4
  7.5 4.1 %all-to-all-start = ((bf16[8,80,512]{2,1,0:T(8,128)(2,1)}), bf16[8,80,512]{2,1,0:T(8,128)(2,1)S(1)}, u32[]{:S(2)}, u32[]{:S(2)}) async-start(bf16[8,80,512]{2,1,0:T(8,128)(2,1)} %pad_maximum_fusion.4), calls=%async_computation | async-start | bytes 1310720 | tf_op jit(solution)/shard_map/all_to_all | solution.py:191
  11.6 0.8 pad_maximum_fusion.6
  12.4 9.4 %all-to-all-done = bf16[8,80,512]{2,1,0:T(8,128)(2,1)S(1)} async-done(((bf16[8,80,512]{2,1,0:T(8,128)(2,1)}), bf16[8,80,512]{2,1,0:T(8,128)(2,1)S(1)}, u32[]{:S(2)}, u32[]{:S(2)}) %all-to-all-start) | async-done | bytes 655392 | tf_op jit(solution)/shard_map/all_to_all | solution.py:191
  21.9 3.5 %all-to-all-start.1 = ((bf16[8,64,512]{2,1,0:T(8,128)(2,1)}), bf16[8,64,512]{2,1,0:T(8,128)(2,1)S(1)}, u32[]{:S(2)}, u32[]{:S(2)}) async-start(bf16[8,64,512]{2,1,0:T(8,128)(2,1)} %bitcast.6), calls=%async_computation.1 | async-start | bytes 1048576 | tf_op jit(solution)/shard_map/all_to_all | solution.py:191
  25.6 0.1 fusion.18
  25.8 0.1 select_reduce_fusion.2
  25.9 0.1 select_reduce_fusion.1
  26.0 0.6 gather_fusion.7
  26.6 4.5 %collective-permute-start.3 = (bf16[4,64,512]{2,1,0:T(8,128)(2,1)S(1)}, bf16[4,64,512]{2,1,0:T(8,128)(2,1)S(1)}, u32[]{:S(2)}, u32[]{:S(2)}) collective-permute-start(bf16[4,64,512]{2,1,0:T(8,128)(2,1)S(1)} %gather_fusion.7), channel_id=1, source_target_pairs={{0,8},{1,9},{2,10},{3,11},{4,12},{5,13},{6,14},{7,15},{16,24},{17,... | collective-permute-start | bytes 786440 | tf_op jit(solution)/shard_map/ppermute | solution.py:232
  31.2 0.1 select_reduce_fusion
  31.3 0.6 convert_reduce_fusion
  32.6 5.1 %collective-permute-done.3 = bf16[4,64,512]{2,1,0:T(8,128)(2,1)S(1)} collective-permute-done((bf16[4,64,512]{2,1,0:T(8,128)(2,1)S(1)}, bf16[4,64,512]{2,1,0:T(8,128)(2,1)S(1)}, u32[]{:S(2)}, u32[]{:S(2)}) %collective-permute-start.3) | collective-permute-done | bytes 262176 | tf_op jit(solution)/shard_map/ppermute | solution.py:232
  37.7 1.7 %conditional.3 = (bf16[16,64,512]{2,1,0:T(8,128)(2,1)}) conditional(s32[]{:T(128)} %convert_element_type.34, (bf16[4,64,512]{2,1,0:T(8,128)(2,1)S(1)}, bf16[8,64,512]{2,1,0:T(8,128)(2,1)S(1)}, s32[16]{0:T(128)S(1)}, pred[16]{0:T(512)(128)(4,1)S(1)}, s32[16]{0:T(128)S(1)}) %tuple.21, (s32[8]{0:T(128)S(1)}, bf16[8,64,512]{2,1,0:T(8,128)(2,1)S(1)}, ...), branch_computations={%region_7.8_spmd, %region_8.9_spmd} | conditional | flops 1050832 | bytes 5775808 | solution.py:243
  37.8 1.6 %gather_fusion.3 = bf16[16,64,512]{2,1,0:T(8,128)(2,1)} fusion(bf16[12,64,512]{2,1,0:T(8,128)(2,1)S(1)} %pad_maximum_fusion.2, s32[1024]{0:T(1024)S(1)} %pad_clamp_fusion.3), kind=kCustom, calls=%fused_computation.3 | custom fusion | bytes 2097216 | tf_op jit(solution)/shard_map/cond/branch_0_fun/jit(_take)/gather | solution.py:241
  39.4 8.9 %all-to-all-start.3 = ((bf16[8,2,64,512]{3,2,1,0:T(8,128)(2,1)}), bf16[8,2,64,512]{3,2,1,0:T(8,128)(2,1)S(1)}, u32[]{:S(2)}, u32[]{:S(2)}) async-start(bf16[8,2,64,512]{3,2,1,0:T(8,128)(2,1)} %bitcast.8), calls=%async_computation.3 | async-start | bytes 2097152 | tf_op jit(solution)/shard_map/all_to_all | solution.py:191
  48.3 0.6 gather_fusion.6
  48.9 5.3 %collective-permute-start.4 = (bf16[4,64,512]{2,1,0:T(8,128)(2,1)S(1)}, bf16[4,64,512]{2,1,0:T(8,128)(2,1)S(1)}, u32[]{:S(2)}, u32[]{:S(2)}) collective-permute-start(bf16[4,64,512]{2,1,0:T(8,128)(2,1)S(1)} %gather_fusion.6), channel_id=1, source_target_pairs={{0,8},{1,9},{2,10},{3,11},{4,12},{5,13},{6,14},{7,15},{16,24},{17,... | collective-permute-start | bytes 786440 | tf_op jit(solution)/shard_map/ppermute | solution.py:232
  54.2 12.1 %collective-permute-done.4 = bf16[4,64,512]{2,1,0:T(8,128)(2,1)S(1)} collective-permute-done((bf16[4,64,512]{2,1,0:T(8,128)(2,1)S(1)}, bf16[4,64,512]{2,1,0:T(8,128)(2,1)S(1)}, u32[]{:S(2)}, u32[]{:S(2)}) %collective-permute-start.4) | collective-permute-done | bytes 262176 | tf_op jit(solution)/shard_map/ppermute | solution.py:232
  66.3 1.7 %conditional.2 = (bf16[16,64,512]{2,1,0:T(8,128)(2,1)}) conditional(s32[]{:T(128)} %convert_element_type.34, (bf16[4,64,512]{2,1,0:T(8,128)(2,1)S(1)}, bf16[8,64,512]{2,1,0:T(8,128)(2,1)S(1)}, s32[16]{0:T(128)S(1)}, pred[16]{0:T(512)(128)(4,1)S(1)}, s32[16]{0:T(128)S(1)}) %tuple.19, (s32[8]{0:T(128)S(1)}, bf16[8,64,512]{2,1,0:T(8,128)(2,1)S(1)}, ...), branch_computations={%region_5.6_spmd, %region_6.7_spmd} | conditional | flops 1050832 | bytes 5775808 | solution.py:243
  66.4 1.6 %gather_fusion = bf16[16,64,512]{2,1,0:T(8,128)(2,1)} fusion(bf16[12,64,512]{2,1,0:T(8,128)(2,1)S(1)} %pad_maximum_fusion, s32[1024]{0:T(1024)S(1)} %pad_clamp_fusion), kind=kCustom, calls=%fused_computation | custom fusion | bytes 2097216 | tf_op jit(solution)/shard_map/cond/branch_0_fun/jit(_take)/gather | solution.py:241
  68.0 3.6 %all-to-all-start.2 = ((bf16[8,2,64,512]{3,2,1,0:T(8,128)(2,1)}), bf16[8,2,64,512]{3,2,1,0:T(8,128)(2,1)S(1)}, u32[]{:S(2)}, u32[]{:S(2)}) async-start(bf16[8,2,64,512]{3,2,1,0:T(8,128)(2,1)} %bitcast.7), calls=%async_computation.2 | async-start | bytes 2097152 | tf_op jit(solution)/shard_map/all_to_all | solution.py:191
  71.6 7.5 %shard_map.47.kept_ref = f32[16,136,512]{2,1,0:T(8,128)} custom-call(bf16[512,4096]{1,0:T(8,128)(2,1)} %q_ref.7, bf16[512,512]{1,0:T(8,128)(2,1)} %k_ref.3, bf16[512,512]{1,0:T(8,128)(2,1)} %v_ref.3), custom_call_target="tpu_custom_call" | custom-call | flops 2147483648 | bytes 4456448 | tf_op jit(solution)/shard_map/pallas_call | solution.py:83
  79.1 7.3 %shard_map.46.kept_ref = f32[16,136,512]{2,1,0:T(8,128)} custom-call(bf16[512,4096]{1,0:T(8,128)(2,1)} %q_ref.7, bf16[512,512]{1,0:T(8,128)(2,1)} %k_ref.3, bf16[512,512]{1,0:T(8,128)(2,1)} %v_ref.3), custom_call_target="tpu_custom_call" | custom-call | flops 2147483648 | bytes 4456448 | tf_op jit(solution)/shard_map/pallas_call | solution.py:83
  86.4 0.5 compare_select_fusion.8.dead_ref
  86.9 14.2 %shard_map.48.rest_0_ = bf16[512,4096]{1,0:T(8,128)(2,1)} custom-call(f32[2]{0:T(128)} %compare_select_fusion.8.dead_ref, bf16[512,4096]{1,0:T(8,128)(2,1)} %q_ref.7, f32[16,136,512]{2,1,0:T(8,128)} %shard_map.47.kept_ref, bf16[8,2,64,512]{3,2,1,0:T(8,128)(2,1)} %copy-done.1, bf16[8,2,64,512]{3,2,1,0:T(8,128)(2,1)} %copy-done.1), custom_call_target="tpu_custom_call" | custom-call | flops 4294967296 | bytes 8388608 | tf_op jit(solution)/shard_map/pallas_call | solution.py:164
  101.2 1.0 copy-done
  102.2 14.3 %shard_map.49 = bf16[512,4096]{1,0:T(8,128)(2,1)} custom-call(f32[2]{0:T(128)} %compare_select_fusion.8.dead_ref, bf16[512,4096]{1,0:T(8,128)(2,1)} %q_ref.7, f32[16,136,512]{2,1,0:T(8,128)} %shard_map.46.kept_ref, bf16[8,2,64,512]{3,2,1,0:T(8,128)(2,1)} %copy-done, bf16[8,2,64,512]{3,2,1,0:T(8,128)(2,1)} %copy-done, ...), custom_call_target="tpu_custom_call", output_to_operand_aliasing={{}: (5, {})} | custom-call | flops 4294967296 | bytes 8388608 | tf_op jit(solution)/shard_map/pallas_call | solution.py:164
  (28 shorter events, 0.7 us)
Async XLA Ops:
  0.0 5.7 %collective-permute-start.2 = (s32[1,2]{1,0:T(1,128)}, s32[1,2]{1,0:T(1,128)S(1)}, u32[]{:S(2)}, u32[]{:S(2)}) collective-permute-start(s32[1,2]{1,0:T(1,128)} %param.11), channel_id=1, source_target_pairs={{0,8},{8,0},{1,9},{9,1},{2,10},{10,2},{3,11},{11,3},{4,12},{12,4},... | collective-permute-start | bytes 32 | tf_op jit(solution)/shard_map/ppermute | solution.py:196
  7.5 14.4 %all-to-all-start = ((bf16[8,80,512]{2,1,0:T(8,128)(2,1)}), bf16[8,80,512]{2,1,0:T(8,128)(2,1)S(1)}, u32[]{:S(2)}, u32[]{:S(2)}) async-start(bf16[8,80,512]{2,1,0:T(8,128)(2,1)} %pad_maximum_fusion.4), calls=%async_computation | async-start | bytes 1310720 | tf_op jit(solution)/shard_map/all_to_all | solution.py:191
  21.9 17.5 %all-to-all-start.1 = ((bf16[8,64,512]{2,1,0:T(8,128)(2,1)}), bf16[8,64,512]{2,1,0:T(8,128)(2,1)S(1)}, u32[]{:S(2)}, u32[]{:S(2)}) async-start(bf16[8,64,512]{2,1,0:T(8,128)(2,1)} %bitcast.6), calls=%async_computation.1 | async-start | bytes 1048576 | tf_op jit(solution)/shard_map/all_to_all | solution.py:191
  26.6 11.2 %collective-permute-start.3 = (bf16[4,64,512]{2,1,0:T(8,128)(2,1)S(1)}, bf16[4,64,512]{2,1,0:T(8,128)(2,1)S(1)}, u32[]{:S(2)}, u32[]{:S(2)}) collective-permute-start(bf16[4,64,512]{2,1,0:T(8,128)(2,1)S(1)} %gather_fusion.7), channel_id=1, source_target_pairs={{0,8},{1,9},{2,10},{3,11},{4,12},{5,13},{6,14},{7,15},{16,24},{17,... | collective-permute-start | bytes 786440 | tf_op jit(solution)/shard_map/ppermute | solution.py:232
  39.4 28.6 %all-to-all-start.3 = ((bf16[8,2,64,512]{3,2,1,0:T(8,128)(2,1)}), bf16[8,2,64,512]{3,2,1,0:T(8,128)(2,1)S(1)}, u32[]{:S(2)}, u32[]{:S(2)}) async-start(bf16[8,2,64,512]{3,2,1,0:T(8,128)(2,1)} %bitcast.8), calls=%async_computation.3 | async-start | bytes 2097152 | tf_op jit(solution)/shard_map/all_to_all | solution.py:191
  48.9 17.4 %collective-permute-start.4 = (bf16[4,64,512]{2,1,0:T(8,128)(2,1)S(1)}, bf16[4,64,512]{2,1,0:T(8,128)(2,1)S(1)}, u32[]{:S(2)}, u32[]{:S(2)}) collective-permute-start(bf16[4,64,512]{2,1,0:T(8,128)(2,1)S(1)} %gather_fusion.6), channel_id=1, source_target_pairs={{0,8},{1,9},{2,10},{3,11},{4,12},{5,13},{6,14},{7,15},{16,24},{17,... | collective-permute-start | bytes 786440 | tf_op jit(solution)/shard_map/ppermute | solution.py:232
  68.0 11.0 %copy-start.1 = (bf16[8,2,64,512]{3,2,1,0:T(8,128)(2,1)}, bf16[8,2,64,512]{3,2,1,0:T(8,128)(2,1)S(1)}, u32[]{:S(2)}) copy-start(bf16[8,2,64,512]{3,2,1,0:T(8,128)(2,1)S(1)} %all-to-all-done.3.ks_ref.vs_ref) | copy-start | bytes 3145732
  68.0 33.1 %all-to-all-start.2 = ((bf16[8,2,64,512]{3,2,1,0:T(8,128)(2,1)}), bf16[8,2,64,512]{3,2,1,0:T(8,128)(2,1)S(1)}, u32[]{:S(2)}, u32[]{:S(2)}) async-start(bf16[8,2,64,512]{3,2,1,0:T(8,128)(2,1)} %bitcast.7), calls=%async_computation.2 | async-start | bytes 2097152 | tf_op jit(solution)/shard_map/all_to_all | solution.py:191
  79.1 7.4 %copy-start.2 = (s32[1,2]{1,0:T(1,128)S(1)}, s32[1,2]{1,0:T(1,128)}, u32[]{:S(2)}) copy-start(s32[1,2]{1,0:T(1,128)} %param.11) | copy-start | bytes 28
  101.2 1.0 copy-start

commit v4 on v3

--- a/solution.py
+++ b/solution.py
@@ -22,6 +22,7 @@
 DIGIT = 128
 CHUNKS = ((0, 1), (2, 3))
 HEADS = 4
+SLOT_HEADS = 8
 NT = (((1,), (1,)), ((), ()))
 
 
@@ -139,18 +140,18 @@
         row_total = kept_ref[h, HD : HD + 1, at] * shrink + total[HD : HD + 1]
         out_ref[piece(unit)] = (mixture * (1.0 / row_total)).T.astype(jnp.bfloat16)
 
-    staggered(units_of(HEADS), scores, weigh, finish)
+    staggered(units_of(SLOT_HEADS), scores, weigh, finish)
 
 
 def attend_slots(dead, queries, kept, arrived, heads, previous):
     sources, _, stripe, _ = arrived.shape
     count, first = len(heads), heads[0]
-    steps = GROUP // HEADS
+    steps = GROUP // SLOT_HEADS
     block = (sources, TOPK, stripe, HD)
     in_specs = [
         pl.BlockSpec(memory_space=pltpu.SMEM),
-        pl.BlockSpec((BLOCK, HEADS * HD), lambda g, h: (0, (first + g) * steps + h)),
-        pl.BlockSpec((HEADS, KEPT, BLOCK), lambda g, h: (g * steps + h, 0, 0)),
+        pl.BlockSpec((BLOCK, SLOT_HEADS * HD), lambda g, h: (0, (first + g) * steps + h)),
+        pl.BlockSpec((SLOT_HEADS, KEPT, BLOCK), lambda g, h: (g * steps + h, 0, 0)),
         pl.BlockSpec(block, lambda g, h: (0, 0, 0, g)),
         pl.BlockSpec(block, lambda g, h: (0, 0, 0, count + g)),
     ]
@@ -166,7 +167,7 @@
         out_shape=jax.ShapeDtypeStruct(queries.shape, jnp.bfloat16),
         grid=(count, steps),
         in_specs=in_specs,
-        out_specs=pl.BlockSpec((BLOCK, HEADS * HD), lambda g, h: (0, (first + g) * steps + h)),
+        out_specs=pl.BlockSpec((BLOCK, SLOT_HEADS * HD), lambda g, h: (0, (first + g) * steps + h)),
         scratch_shapes=[
             pltpu.VMEM((TOPK * BLOCK, HD), jnp.bfloat16),
             pltpu.VMEM((HD + ONES, TOPK * BLOCK), jnp.bfloat16),

time: 117 us -> 116 us (level)
  no operation moved by 1% of the time
where the time goes in v4:
time: 116 us; the launch traced here: 115 us
  Pallas kernels  42.2 us (36%)
  starting transfers between devices  34 us (29%)
  waiting for transfers between devices  27.1 us (23%)
  local copies, waits for them, and re-layouts  6.77 us (6%)
  other arithmetic  4.48 us (4%)
    pallas_call x2, Pallas kernels, attend_slots(): pl.pallas_call(slots_kernel, out_shape=jax.ShapeDtypeStruct(queries.shape...  27.4 us
    all_to_all x4, starting transfers between devices, exchange(): return lax.all_to_all(x, 'peer', split_axis=0, concat_axis=0, tiled=True)  20.1 us
    ppermute x2, waiting for transfers between devices, whole(): first = lax.ppermute(front, 'half', [(0, 1)])  17.3 us
    pallas_call x2, Pallas kernels, attend_own(): pl.pallas_call(own_kernel, out_shape=jax.ShapeDtypeStruct((GROUP * count,...  14.8 us
    ppermute x2, starting transfers between devices, whole(): first = lax.ppermute(front, 'half', [(0, 1)])  9.81 us
    all_to_all x4, waiting for transfers between devices, exchange(): return lax.all_to_all(x, 'peer', split_axis=0, concat_axis=0, tiled=True)  9.44 us
    ppermute x1, starting transfers between devices, whole(): twin = lax.ppermute(selected, 'half', [(0, 1), (1, 0)])  4.06 us
    gather x2, local copies, waits for them, and re-layouts, few_crossed(): jnp.take(table, jnp.where(near, room + asked % peers, turn), axis=0, mode...  3.17 us
  transfers between devices with their start and end apart: 7, of which 4 were waited for; matrix products, arithmetic and copies ran while one was open for 7% of the time, Pallas kernels for 25%

profile of v4, /device:TPU:0, one launch (start us, length us, event | category | flops | bytes accessed | tf_op | source)
XLA Modules:
  0.0 115.3 jit_solution(14391579451614142877)
XLA Ops:
  0.0 4.1 %collective-permute-start.2 = (s32[1,2]{1,0:T(1,128)}, s32[1,2]{1,0:T(1,128)S(1)}, u32[]{:S(2)}, u32[]{:S(2)}) collective-permute-start(s32[1,2]{1,0:T(1,128)} %param.11), channel_id=1, source_target_pairs={{0,8},{8,0},{1,9},{9,1},{2,10},{10,2},{3,11},{11,3},{4,12},{12,4},... | collective-permute-start | bytes 32 | tf_op jit(solution)/shard_map/ppermute | solution.py:197
  4.1 1.3 %fusion.23 = (bf16[512,256]{1,0:T(8,128)(2,1)S(1)}, bf16[512,256]{1,0:T(8,128)(2,1)S(1)}, bf16[512,256]{1,0:T(8,128)(2,1)S(1)}, bf16[512,256]{1,0:T(8,128)(2,1)S(1)}) fusion(bf16[512,512]{1,0:T(8,128)(2,1)} %k_ref.3, bf16[512,512]{1,0:T(8,128)(2,1)} %v_ref.3), kind=kLoop, calls=%fused_computation.84 | loop fusion | bytes 2097152 | tf_op jit(solution)/shard_map/slice | solution.py:195
  5.4 0.4 collective-permute-done.2
  5.7 0.7 convert_bitcast_fusion
  6.6 0.9 pad_maximum_fusion.4
  7.5 4.1 %all-to-all-start = ((bf16[8,80,512]{2,1,0:T(8,128)(2,1)}), bf16[8,80,512]{2,1,0:T(8,128)(2,1)S(1)}, u32[]{:S(2)}, u32[]{:S(2)}) async-start(bf16[8,80,512]{2,1,0:T(8,128)(2,1)} %pad_maximum_fusion.4), calls=%async_computation | async-start | bytes 1310720 | tf_op jit(solution)/shard_map/all_to_all | solution.py:192
  11.6 0.8 pad_maximum_fusion.6
  12.4 9.4 %all-to-all-done = bf16[8,80,512]{2,1,0:T(8,128)(2,1)S(1)} async-done(((bf16[8,80,512]{2,1,0:T(8,128)(2,1)}), bf16[8,80,512]{2,1,0:T(8,128)(2,1)S(1)}, u32[]{:S(2)}, u32[]{:S(2)}) %all-to-all-start) | async-done | bytes 655392 | tf_op jit(solution)/shard_map/all_to_all | solution.py:192
  21.9 3.5 %all-to-all-start.1 = ((bf16[8,64,512]{2,1,0:T(8,128)(2,1)}), bf16[8,64,512]{2,1,0:T(8,128)(2,1)S(1)}, u32[]{:S(2)}, u32[]{:S(2)}) async-start(bf16[8,64,512]{2,1,0:T(8,128)(2,1)} %bitcast.6), calls=%async_computation.1 | async-start | bytes 1048576 | tf_op jit(solution)/shard_map/all_to_all | solution.py:192
  25.6 0.1 fusion.18
  25.8 0.1 select_reduce_fusion.2
  25.9 0.1 select_reduce_fusion.1
  26.0 0.6 gather_fusion.7
  26.6 4.5 %collective-permute-start.3 = (bf16[4,64,512]{2,1,0:T(8,128)(2,1)S(1)}, bf16[4,64,512]{2,1,0:T(8,128)(2,1)S(1)}, u32[]{:S(2)}, u32[]{:S(2)}) collective-permute-start(bf16[4,64,512]{2,1,0:T(8,128)(2,1)S(1)} %gather_fusion.7), channel_id=1, source_target_pairs={{0,8},{1,9},{2,10},{3,11},{4,12},{5,13},{6,14},{7,15},{16,24},{17,... | collective-permute-start | bytes 786440 | tf_op jit(solution)/shard_map/ppermute | solution.py:233
  31.2 0.1 select_reduce_fusion
  31.3 0.6 convert_reduce_fusion
  32.6 5.1 %collective-permute-done.3 = bf16[4,64,512]{2,1,0:T(8,128)(2,1)S(1)} collective-permute-done((bf16[4,64,512]{2,1,0:T(8,128)(2,1)S(1)}, bf16[4,64,512]{2,1,0:T(8,128)(2,1)S(1)}, u32[]{:S(2)}, u32[]{:S(2)}) %collective-permute-start.3) | collective-permute-done | bytes 262176 | tf_op jit(solution)/shard_map/ppermute | solution.py:233
  37.7 1.7 %conditional.3 = (bf16[16,64,512]{2,1,0:T(8,128)(2,1)}) conditional(s32[]{:T(128)} %convert_element_type.34, (bf16[4,64,512]{2,1,0:T(8,128)(2,1)S(1)}, bf16[8,64,512]{2,1,0:T(8,128)(2,1)S(1)}, s32[16]{0:T(128)S(1)}, pred[16]{0:T(512)(128)(4,1)S(1)}, s32[16]{0:T(128)S(1)}) %tuple.21, (s32[8]{0:T(128)S(1)}, bf16[8,64,512]{2,1,0:T(8,128)(2,1)S(1)}, ...), branch_computations={%region_7.8_spmd, %region_8.9_spmd} | conditional | flops 1050832 | bytes 5775808 | solution.py:244
  37.8 1.6 %gather_fusion.3 = bf16[16,64,512]{2,1,0:T(8,128)(2,1)} fusion(bf16[12,64,512]{2,1,0:T(8,128)(2,1)S(1)} %pad_maximum_fusion.2, s32[1024]{0:T(1024)S(1)} %pad_clamp_fusion.3), kind=kCustom, calls=%fused_computation.3 | custom fusion | bytes 2097216 | tf_op jit(solution)/shard_map/cond/branch_0_fun/jit(_take)/gather | solution.py:242
  39.4 8.9 %all-to-all-start.3 = ((bf16[8,2,64,512]{3,2,1,0:T(8,128)(2,1)}), bf16[8,2,64,512]{3,2,1,0:T(8,128)(2,1)S(1)}, u32[]{:S(2)}, u32[]{:S(2)}) async-start(bf16[8,2,64,512]{3,2,1,0:T(8,128)(2,1)} %bitcast.8), calls=%async_computation.3 | async-start | bytes 2097152 | tf_op jit(solution)/shard_map/all_to_all | solution.py:192
  48.3 0.6 gather_fusion.6
  48.9 5.3 %collective-permute-start.4 = (bf16[4,64,512]{2,1,0:T(8,128)(2,1)S(1)}, bf16[4,64,512]{2,1,0:T(8,128)(2,1)S(1)}, u32[]{:S(2)}, u32[]{:S(2)}) collective-permute-start(bf16[4,64,512]{2,1,0:T(8,128)(2,1)S(1)} %gather_fusion.6), channel_id=1, source_target_pairs={{0,8},{1,9},{2,10},{3,11},{4,12},{5,13},{6,14},{7,15},{16,24},{17,... | collective-permute-start | bytes 786440 | tf_op jit(solution)/shard_map/ppermute | solution.py:233
  54.2 12.1 %collective-permute-done.4 = bf16[4,64,512]{2,1,0:T(8,128)(2,1)S(1)} collective-permute-done((bf16[4,64,512]{2,1,0:T(8,128)(2,1)S(1)}, bf16[4,64,512]{2,1,0:T(8,128)(2,1)S(1)}, u32[]{:S(2)}, u32[]{:S(2)}) %collective-permute-start.4) | collective-permute-done | bytes 262176 | tf_op jit(solution)/shard_map/ppermute | solution.py:233
  66.3 1.7 %conditional.2 = (bf16[16,64,512]{2,1,0:T(8,128)(2,1)}) conditional(s32[]{:T(128)} %convert_element_type.34, (bf16[4,64,512]{2,1,0:T(8,128)(2,1)S(1)}, bf16[8,64,512]{2,1,0:T(8,128)(2,1)S(1)}, s32[16]{0:T(128)S(1)}, pred[16]{0:T(512)(128)(4,1)S(1)}, s32[16]{0:T(128)S(1)}) %tuple.19, (s32[8]{0:T(128)S(1)}, bf16[8,64,512]{2,1,0:T(8,128)(2,1)S(1)}, ...), branch_computations={%region_5.6_spmd, %region_6.7_spmd} | conditional | flops 1050832 | bytes 5775808 | solution.py:244
  66.4 1.6 %gather_fusion = bf16[16,64,512]{2,1,0:T(8,128)(2,1)} fusion(bf16[12,64,512]{2,1,0:T(8,128)(2,1)S(1)} %pad_maximum_fusion, s32[1024]{0:T(1024)S(1)} %pad_clamp_fusion), kind=kCustom, calls=%fused_computation | custom fusion | bytes 2097216 | tf_op jit(solution)/shard_map/cond/branch_0_fun/jit(_take)/gather | solution.py:242
  68.0 3.6 %all-to-all-start.2 = ((bf16[8,2,64,512]{3,2,1,0:T(8,128)(2,1)}), bf16[8,2,64,512]{3,2,1,0:T(8,128)(2,1)S(1)}, u32[]{:S(2)}, u32[]{:S(2)}) async-start(bf16[8,2,64,512]{3,2,1,0:T(8,128)(2,1)} %bitcast.7), calls=%async_computation.2 | async-start | bytes 2097152 | tf_op jit(solution)/shard_map/all_to_all | solution.py:192
  71.6 7.5 %shard_map.47.kept_ref = f32[16,136,512]{2,1,0:T(8,128)} custom-call(bf16[512,4096]{1,0:T(8,128)(2,1)} %q_ref.7, bf16[512,512]{1,0:T(8,128)(2,1)} %k_ref.3, bf16[512,512]{1,0:T(8,128)(2,1)} %v_ref.3), custom_call_target="tpu_custom_call" | custom-call | flops 2147483648 | bytes 4456448 | tf_op jit(solution)/shard_map/pallas_call | solution.py:84
  79.1 7.3 %shard_map.46.kept_ref = f32[16,136,512]{2,1,0:T(8,128)} custom-call(bf16[512,4096]{1,0:T(8,128)(2,1)} %q_ref.7, bf16[512,512]{1,0:T(8,128)(2,1)} %k_ref.3, bf16[512,512]{1,0:T(8,128)(2,1)} %v_ref.3), custom_call_target="tpu_custom_call" | custom-call | flops 2147483648 | bytes 4456448 | tf_op jit(solution)/shard_map/pallas_call | solution.py:84
  86.4 0.5 compare_select_fusion.8.dead_ref
  86.9 13.7 %shard_map.48.rest_0_ = bf16[512,4096]{1,0:T(8,128)(2,1)} custom-call(f32[2]{0:T(128)} %compare_select_fusion.8.dead_ref, bf16[512,4096]{1,0:T(8,128)(2,1)} %q_ref.7, f32[16,136,512]{2,1,0:T(8,128)} %shard_map.47.kept_ref, bf16[8,2,64,512]{3,2,1,0:T(8,128)(2,1)} %copy-done.1, bf16[8,2,64,512]{3,2,1,0:T(8,128)(2,1)} %copy-done.1), custom_call_target="tpu_custom_call" | custom-call | flops 4294967296 | bytes 8388608 | tf_op jit(solution)/shard_map/pallas_call | solution.py:165
  100.6 1.0 copy-done
  101.6 13.7 %shard_map.49 = bf16[512,4096]{1,0:T(8,128)(2,1)} custom-call(f32[2]{0:T(128)} %compare_select_fusion.8.dead_ref, bf16[512,4096]{1,0:T(8,128)(2,1)} %q_ref.7, f32[16,136,512]{2,1,0:T(8,128)} %shard_map.46.kept_ref, bf16[8,2,64,512]{3,2,1,0:T(8,128)(2,1)} %copy-done, bf16[8,2,64,512]{3,2,1,0:T(8,128)(2,1)} %copy-done, ...), custom_call_target="tpu_custom_call", output_to_operand_aliasing={{}: (5, {})} | custom-call | flops 4294967296 | bytes 8388608 | tf_op jit(solution)/shard_map/pallas_call | solution.py:165
  (28 shorter events, 0.7 us)
Async XLA Ops:
  0.0 5.7 %collective-permute-start.2 = (s32[1,2]{1,0:T(1,128)}, s32[1,2]{1,0:T(1,128)S(1)}, u32[]{:S(2)}, u32[]{:S(2)}) collective-permute-start(s32[1,2]{1,0:T(1,128)} %param.11), channel_id=1, source_target_pairs={{0,8},{8,0},{1,9},{9,1},{2,10},{10,2},{3,11},{11,3},{4,12},{12,4},... | collective-permute-start | bytes 32 | tf_op jit(solution)/shard_map/ppermute | solution.py:197
  7.5 14.4 %all-to-all-start = ((bf16[8,80,512]{2,1,0:T(8,128)(2,1)}), bf16[8,80,512]{2,1,0:T(8,128)(2,1)S(1)}, u32[]{:S(2)}, u32[]{:S(2)}) async-start(bf16[8,80,512]{2,1,0:T(8,128)(2,1)} %pad_maximum_fusion.4), calls=%async_computation | async-start | bytes 1310720 | tf_op jit(solution)/shard_map/all_to_all | solution.py:192
  21.9 17.5 %all-to-all-start.1 = ((bf16[8,64,512]{2,1,0:T(8,128)(2,1)}), bf16[8,64,512]{2,1,0:T(8,128)(2,1)S(1)}, u32[]{:S(2)}, u32[]{:S(2)}) async-start(bf16[8,64,512]{2,1,0:T(8,128)(2,1)} %bitcast.6), calls=%async_computation.1 | async-start | bytes 1048576 | tf_op jit(solution)/shard_map/all_to_all | solution.py:192
  26.6 11.2 %collective-permute-start.3 = (bf16[4,64,512]{2,1,0:T(8,128)(2,1)S(1)}, bf16[4,64,512]{2,1,0:T(8,128)(2,1)S(1)}, u32[]{:S(2)}, u32[]{:S(2)}) collective-permute-start(bf16[4,64,512]{2,1,0:T(8,128)(2,1)S(1)} %gather_fusion.7), channel_id=1, source_target_pairs={{0,8},{1,9},{2,10},{3,11},{4,12},{5,13},{6,14},{7,15},{16,24},{17,... | collective-permute-start | bytes 786440 | tf_op jit(solution)/shard_map/ppermute | solution.py:233
  39.4 28.6 %all-to-all-start.3 = ((bf16[8,2,64,512]{3,2,1,0:T(8,128)(2,1)}), bf16[8,2,64,512]{3,2,1,0:T(8,128)(2,1)S(1)}, u32[]{:S(2)}, u32[]{:S(2)}) async-start(bf16[8,2,64,512]{3,2,1,0:T(8,128)(2,1)} %bitcast.8), calls=%async_computation.3 | async-start | bytes 2097152 | tf_op jit(solution)/shard_map/all_to_all | solution.py:192
  48.9 17.4 %collective-permute-start.4 = (bf16[4,64,512]{2,1,0:T(8,128)(2,1)S(1)}, bf16[4,64,512]{2,1,0:T(8,128)(2,1)S(1)}, u32[]{:S(2)}, u32[]{:S(2)}) collective-permute-start(bf16[4,64,512]{2,1,0:T(8,128)(2,1)S(1)} %gather_fusion.6), channel_id=1, source_target_pairs={{0,8},{1,9},{2,10},{3,11},{4,12},{5,13},{6,14},{7,15},{16,24},{17,... | collective-permute-start | bytes 786440 | tf_op jit(solution)/shard_map/ppermute | solution.py:233
  68.0 11.0 %copy-start.1 = (bf16[8,2,64,512]{3,2,1,0:T(8,128)(2,1)}, bf16[8,2,64,512]{3,2,1,0:T(8,128)(2,1)S(1)}, u32[]{:S(2)}) copy-start(bf16[8,2,64,512]{3,2,1,0:T(8,128)(2,1)S(1)} %all-to-all-done.3.ks_ref.vs_ref) | copy-start | bytes 3145732
  68.0 32.6 %all-to-all-start.2 = ((bf16[8,2,64,512]{3,2,1,0:T(8,128)(2,1)}), bf16[8,2,64,512]{3,2,1,0:T(8,128)(2,1)S(1)}, u32[]{:S(2)}, u32[]{:S(2)}) async-start(bf16[8,2,64,512]{3,2,1,0:T(8,128)(2,1)} %bitcast.7), calls=%async_computation.2 | async-start | bytes 2097152 | tf_op jit(solution)/shard_map/all_to_all | solution.py:192
  79.1 7.4 %copy-start.2 = (s32[1,2]{1,0:T(1,128)S(1)}, s32[1,2]{1,0:T(1,128)}, u32[]{:S(2)}) copy-start(s32[1,2]{1,0:T(1,128)} %param.11) | copy-start | bytes 28
  100.6 1.0 copy-start
